TPU v7x, 128 devices: a whole 4x4x4 slice. The times are simulated.
128 devices in a mesh: segment: 4 (over y), lane: 32 (over x, z, core).
Axes of the slice: x: 4, y: 4, z: 4, core: 2. Of those that a mesh axis runs over, the one named last changes fastest.
Arguments:
- frames: bfloat16 [96, 197, 1024], P('lane'), may hold values from -6 to 6
- triple_weight: bfloat16 [4, 1024, 3072], P('segment'), as said below
- output_weight: bfloat16 [4, 1024, 1024], P('segment'), may hold values from -0.1875 to 0.1875
- expand_weight: bfloat16 [4, 1024, 4096], P('segment', None, 'lane'), may hold values from -0.1875 to 0.1875
- reduce_weight: bfloat16 [4, 4096, 1024], P('segment', 'lane'), may hold values from -0.09375 to 0.09375
- attend_gain: float32 [4, 1024], P('segment'), may hold values from 0.1 to 1.9
- dense_gain: float32 [4, 1024], P('segment'), may hold values from 0.1 to 1.9
- final_gain: float32 [1024], replicated, may hold values from 0.1 to 1.9
- shot_lengths: int32 [24], replicated, may hold values from 1 to 12, as said below
Outputs:
- shot_frames: float32 [96, 1024], P('lane', 'segment')
Inputs may be any that keep to these rules, and one draw needn't show every extreme that they name: `shot_lengths`: each shot is a run of consecutive frames; the lengths sum to 96; the first shot has 2 frames and the second exactly 12. `triple_weight`: query and value columns are drawn like a weight with fan-in 1024; key columns may be up to 60 times that scale and correlated with the query columns.
All inputs are finite; a program needn't handle non-finite values.
Results may differ from a plain program's by a relative error of at most 0.023.
Values may be sent and summed in bfloat16 or wider, within the bound.
A program may use at most 128 MiB of HBM per device.

v0:
```python
import math

import jax
import jax.numpy as jnp
from jax import lax
from jax.sharding import PartitionSpec as P

HEADS = 16
MOST = 12


def from_behind(value, axis, steps):
    count = lax.axis_size(axis)
    leading, last = (max(0, -steps), min(count, count - steps))
    return lax.ppermute(value, axis, [(source, source + steps) for source in range(leading, last)])


def normalize(states, gain_row):
    average = jnp.mean(states, axis=-1, keepdims=True)
    centred = states - average
    spread = jnp.mean(centred * centred, axis=-1, keepdims=True)
    return centred * lax.rsqrt(spread + 1e-06) * gain_row


def spatial_layer(
    states, triple_weight, output_weight, expand_weight, reduce_weight, attend_gain, dense_gain
):
    group_size, row_count, model_width = states.shape
    head_size = model_width // HEADS
    normed = normalize(states, attend_gain).astype(jnp.bfloat16)
    packed = jnp.einsum(
        "gpd,de->gpe", normed, triple_weight, preferred_element_type=jnp.float32
    ).astype(jnp.bfloat16)
    packed = packed.reshape(group_size, row_count, 3, HEADS, head_size)
    scores = jnp.einsum(
        "gqhe,gkhe->ghqk", packed[:, :, 0], packed[:, :, 1], preferred_element_type=jnp.float32
    ) / math.sqrt(head_size)
    weights = jax.nn.softmax(scores, axis=-1).astype(jnp.bfloat16)
    context = jnp.einsum(
        "ghqk,gkhe->gqhe", weights, packed[:, :, 2], preferred_element_type=jnp.float32
    )
    context = context.astype(jnp.bfloat16).reshape(group_size, row_count, model_width)
    states = states + jnp.einsum(
        "gpd,de->gpe", context, output_weight, preferred_element_type=jnp.float32
    )
    normed = normalize(states, dense_gain).astype(jnp.bfloat16)
    hidden = jax.nn.gelu(
        jnp.einsum("gpd,df->gpf", normed, expand_weight, preferred_element_type=jnp.float32),
        approximate=False,
    ).astype(jnp.bfloat16)
    return states + jnp.einsum(
        "gpf,fd->gpd", hidden, reduce_weight, preferred_element_type=jnp.float32
    )


def shot_number(positions, shot_ends):
    return jnp.sum((shot_ends[None, :] <= positions[:, None]).astype(jnp.int32), axis=1)


def fold_keys(running, portion, first_row, queries, query_shot, shot_ends, frame_total):
    highest, totals, weighted = running
    row_count = portion.shape[0]
    model_width = portion.shape[1] // 2
    head_size = model_width // HEADS
    key_rows = portion[:, :model_width].reshape(row_count, HEADS, head_size)
    value_rows = portion[:, model_width:].astype(jnp.float32).reshape(row_count, HEADS, head_size)
    positions = first_row + jnp.arange(row_count, dtype=jnp.int32)
    inside = (positions >= 0) & (positions < frame_total)
    allowed = (query_shot[:, None] == shot_number(positions, shot_ends)[None, :]) & inside[None, :]
    scores = jnp.einsum(
        "qhe,khe->hqk", queries, key_rows, preferred_element_type=jnp.float32
    ) / math.sqrt(head_size)
    masked = jnp.where(allowed[None], scores, -1e30)
    raised = jnp.maximum(highest, jnp.max(masked, axis=-1))
    factor = jnp.exp(highest - raised)
    shares = jnp.where(allowed[None], jnp.exp(scores - raised[:, :, None]), 0.0)
    totals = totals * factor + jnp.sum(shares, axis=-1)
    weighted = weighted * jnp.transpose(factor)[:, :, None] + jnp.einsum(
        "hqk,khe->qhe", shares, value_rows, precision=lax.Precision.HIGHEST
    )
    return (raised, totals, weighted)


def body(
    frames,
    triple_weight,
    output_weight,
    expand_weight,
    reduce_weight,
    attend_gain,
    dense_gain,
    final_gain,
    shot_lengths,
):
    segment_index = lax.axis_index("segment")
    segment_count = lax.axis_size("segment")
    lane_index = lax.axis_index("lane")
    lane_count = lax.axis_size("lane")
    frame_count, row_count, model_width = frames.shape
    expand_full, reduce_full = (
        lax.all_gather(expand_weight[0], "lane", axis=1, tiled=True),
        lax.all_gather(reduce_weight[0], "lane", axis=0, tiled=True),
    )
    triple_local = triple_weight[0]
    output_local = output_weight[0]
    attend_local = attend_gain[0]
    dense_local = dense_gain[0]
    group_size = 1
    micro_count = frame_count // group_size

    def advance(moment, running):
        current, pooled = running
        first_frame = jnp.minimum(moment, micro_count - 1) * group_size
        loaded = lax.dynamic_slice_in_dim(frames, first_frame, group_size, 0).astype(jnp.float32)
        current = jnp.where(segment_index == 0, loaded, current)
        result = spatial_layer(
            current, triple_local, output_local, expand_full, reduce_full, attend_local, dense_local
        )
        arrived = from_behind(result, "segment", 1)
        finished = moment - (segment_count - 2)
        summary = jnp.mean(normalize(arrived, final_gain), axis=1)
        slot_row = jnp.clip(finished, 0, micro_count - 1) * group_size
        previous = lax.dynamic_slice_in_dim(pooled, slot_row, group_size, 0)
        updated = jnp.where(finished >= 0, summary, previous)
        return (arrived, lax.dynamic_update_slice_in_dim(pooled, updated, slot_row, 0))

    start_state = (
        jnp.zeros((group_size, row_count, model_width), jnp.float32),
        jnp.zeros((frame_count, model_width), jnp.float32),
    )
    settled, pooled = lax.fori_loop(0, micro_count + segment_count - 2, advance, start_state)
    head_size = model_width // HEADS
    normed = normalize(pooled, attend_local).astype(jnp.bfloat16)
    packed = jnp.dot(normed, triple_local, preferred_element_type=jnp.float32).astype(jnp.bfloat16)
    queries = packed[:, :model_width].reshape(frame_count, HEADS, head_size)
    key_value = packed[:, model_width:]
    shot_ends = jnp.cumsum(shot_lengths)
    frame_total = frame_count * lane_count
    own_rows = lane_index * frame_count + jnp.arange(frame_count, dtype=jnp.int32)
    query_shot = shot_number(own_rows, shot_ends)

    def absorb(running, portion, first_row):
        return fold_keys(running, portion, first_row, queries, query_shot, shot_ends, frame_total)

    empty = (
        jnp.full((HEADS, frame_count), -1e30, jnp.float32),
        jnp.zeros((HEADS, frame_count), jnp.float32),
        jnp.zeros((frame_count, HEADS, head_size), jnp.float32),
    )
    running = absorb(empty, key_value, lane_index * frame_count)
    reach = (MOST + frame_count - 2) // frame_count
    offsets = [direction * distance for distance in range(1, reach + 1) for direction in (1, -1)]
    for offset in offsets:
        portion = from_behind(key_value, "lane", offset)
        running = absorb(running, portion, (lane_index - offset) * frame_count)
    highest, totals, weighted = running
    context = (
        (weighted / jnp.transpose(totals)[:, :, None])
        .reshape(frame_count, model_width)
        .astype(jnp.bfloat16)
    )
    temporal = pooled + jnp.dot(context, output_local, preferred_element_type=jnp.float32)
    normed = normalize(temporal, dense_local).astype(jnp.bfloat16)
    hidden = jax.nn.gelu(
        jnp.dot(normed, expand_full, preferred_element_type=jnp.float32), approximate=False
    ).astype(jnp.bfloat16)
    temporal = temporal + jnp.dot(hidden, reduce_full, preferred_element_type=jnp.float32)
    columns = temporal.reshape(frame_count, segment_count, model_width // segment_count)
    shared = lax.all_to_all(columns, "segment", split_axis=1, concat_axis=1, tiled=True)
    return shared[:, segment_count - 1]


def solution(mesh):
    return jax.shard_map(
        body,
        mesh=mesh,
        in_specs=(
            P("lane", None, None),
            P("segment", None, None),
            P("segment", None, None),
            P("segment", None, "lane"),
            P("segment", "lane", None),
            P("segment", None),
            P("segment", None),
            P(),
            P(),
        ),
        out_specs=P("lane", "segment"),
        check_vma=False,
    )
```

profile of v0, /device:TPU:0, one launch (start us, length us, event | category | flops | bytes accessed | tf_op | source)
XLA Modules:
  0.0 471.6 jit_solution(12670992070367799868)
XLA Ops:
  10.1 61.6 %all-gather.5.cloned.1.call-done = bf16[1,1024,4096]{2,1,0:T(8,128)(2,1)} async-done(((bf16[1,1024,128]{2,1,0:T(8,128)(2,1)}), bf16[1,1024,4096]{2,1,0:T(8,128)(2,1)}) %all-gather.5.cloned.1.call-update) | async-done | bytes 8388624 | tf_op jit(solution)/shard_map/all_gather | solution.py:101
  71.7 54.9 %all-gather.7.cloned.1.call-done = bf16[1,4096,1024]{2,1,0:T(8,128)(2,1)} async-done(((bf16[1,128,1024]{2,1,0:T(8,128)(2,1)}), bf16[1,4096,1024]{2,1,0:T(8,128)(2,1)}) %all-gather.7.cloned.1.call-update) | async-done | bytes 8388624 | tf_op jit(solution)/shard_map/all_gather | solution.py:102
  127.1 282.9 %while.17 = (s32[]{:T(128)}, f32[1,197,1024]{2,0,1:T(1,128)S(1)}, f32[3,1024]{1,0:T(4,128)S(1)}, pred[]{:T(512)}, bf16[3,197,1024]{2,1,0:T(8,128)(2,1)}, /*index...) while((s32[]{:T(128)}, f32[1,197,1024]{2,0,1:T(1,128)S(1)}, ...), condition=%wide.region_10.11_spmd, body=%wide.region_0.10_spmd.sunk | while | flops 5180471808 | bytes 65759924 | solution.py:131
  129.6 5.6 %convolution_convert_fusion.3 = bf16[197,3072]{1,0:T(8,128)(2,1)} fusion(bf16[1024,3072]{1,0:T(8,128)(2,1)} %get-tuple-element.539, f32[1024]{0:T(1024)} %bitcast.303, f32[197]{0:T(256)S(1)} %add_rsqrt_fusion.8, f32[197]{0:T(256)S(1)} %broadcast_multiply_fusion.10, f32[1,197,1024]{2,0,1:T(1,128)S(1)} %get-tuple-element.516, ...), kind=kOutput, calls=%fused_computation.2.clone.1 | convolution fusion | flops 1241232384 | bytes 8724524 | tf_op jit(solution)/shard_map/while/body/eval_jaxpr/gpd,de->gpe/dot_general | solution.py:31
  135.2 1.6 copy.297
  137.5 2.7 fusion.341
  141.8 1.7 fusion.343
  143.8 14.2 %fusion.344 = f32[1,197,1024]{2,1,0:T(8,128)S(1)} fusion(f32[1,197,1024]{2,1,0:T(8,128)S(1)} %get-tuple-element.495, bf16[4096,1024]{1,0:T(8,128)(2,1)} %get-tuple-element.543, bf16[1024,4096]{1,0:T(8,128)(2,1)} %get-tuple-element.542, f32[1024]{0:T(1024)S(1)} %bitcast.305, f32[197]{0:T(256)S(1)} %add_rsqrt_fusion.9, ...), kind=kOutput, calls=%fused_computation.61.clone.1 | convolution fusion | flops 3358569472 | bytes 18396712 | tf_op jit(solution)/shard_map/while/body/eval_jaxpr/gpf,fd->gpd/dot_general | solution.py:51
  158.9 3.4 collective-permute-start
  162.3 17.6 %collective-permute-done = f32[1,197,1024]{2,0,1:T(1,128)S(1)} collective-permute-done((f32[1,197,1024]{2,0,1:T(1,128)S(1)}, f32[1,197,1024]{2,0,1:T(1,128)S(1)}, u32[]{:S(2)}, u32[]{:S(2)}) %collective-permute-start) | collective-permute-done | bytes 806944 | tf_op jit(solution)/shard_map/while/body/eval_jaxpr/ppermute | solution.py:15
  181.0 2.1 multiply_reduce_fusion.13
  187.1 5.6 %convolution_convert_fusion.3 = bf16[197,3072]{1,0:T(8,128)(2,1)} fusion(bf16[1024,3072]{1,0:T(8,128)(2,1)} %get-tuple-element.539, f32[1024]{0:T(1024)} %bitcast.303, f32[197]{0:T(256)S(1)} %add_rsqrt_fusion.8, f32[197]{0:T(256)S(1)} %broadcast_multiply_fusion.10, f32[1,197,1024]{2,0,1:T(1,128)S(1)} %get-tuple-element.516, ...), kind=kOutput, calls=%fused_computation.2.clone.1 | convolution fusion | flops 1241232384 | bytes 8724524 | tf_op jit(solution)/shard_map/while/body/eval_jaxpr/gpd,de->gpe/dot_general | solution.py:31
  195.0 2.7 fusion.341
  199.3 1.7 fusion.343
  201.3 14.2 %fusion.344 = f32[1,197,1024]{2,1,0:T(8,128)S(1)} fusion(f32[1,197,1024]{2,1,0:T(8,128)S(1)} %get-tuple-element.495, bf16[4096,1024]{1,0:T(8,128)(2,1)} %get-tuple-element.543, bf16[1024,4096]{1,0:T(8,128)(2,1)} %get-tuple-element.542, f32[1024]{0:T(1024)S(1)} %bitcast.305, f32[197]{0:T(256)S(1)} %add_rsqrt_fusion.9, ...), kind=kOutput, calls=%fused_computation.61.clone.1 | convolution fusion | flops 3358569472 | bytes 18396712 | tf_op jit(solution)/shard_map/while/body/eval_jaxpr/gpf,fd->gpd/dot_general | solution.py:51
  216.4 4.4 collective-permute-start
  220.8 16.8 %collective-permute-done = f32[1,197,1024]{2,0,1:T(1,128)S(1)} collective-permute-done((f32[1,197,1024]{2,0,1:T(1,128)S(1)}, f32[1,197,1024]{2,0,1:T(1,128)S(1)}, u32[]{:S(2)}, u32[]{:S(2)}) %collective-permute-start) | collective-permute-done | bytes 806944 | tf_op jit(solution)/shard_map/while/body/eval_jaxpr/ppermute | solution.py:15
  238.7 2.1 multiply_reduce_fusion.13
  244.8 5.6 %convolution_convert_fusion.3 = bf16[197,3072]{1,0:T(8,128)(2,1)} fusion(bf16[1024,3072]{1,0:T(8,128)(2,1)} %get-tuple-element.539, f32[1024]{0:T(1024)} %bitcast.303, f32[197]{0:T(256)S(1)} %add_rsqrt_fusion.8, f32[197]{0:T(256)S(1)} %broadcast_multiply_fusion.10, f32[1,197,1024]{2,0,1:T(1,128)S(1)} %get-tuple-element.516, ...), kind=kOutput, calls=%fused_computation.2.clone.1 | convolution fusion | flops 1241232384 | bytes 8724524 | tf_op jit(solution)/shard_map/while/body/eval_jaxpr/gpd,de->gpe/dot_general | solution.py:31
  250.4 1.6 copy.297
  252.7 2.7 fusion.341
  257.0 1.7 fusion.343
  259.0 14.2 %fusion.344 = f32[1,197,1024]{2,1,0:T(8,128)S(1)} fusion(f32[1,197,1024]{2,1,0:T(8,128)S(1)} %get-tuple-element.495, bf16[4096,1024]{1,0:T(8,128)(2,1)} %get-tuple-element.543, bf16[1024,4096]{1,0:T(8,128)(2,1)} %get-tuple-element.542, f32[1024]{0:T(1024)S(1)} %bitcast.305, f32[197]{0:T(256)S(1)} %add_rsqrt_fusion.9, ...), kind=kOutput, calls=%fused_computation.61.clone.1 | convolution fusion | flops 3358569472 | bytes 18396712 | tf_op jit(solution)/shard_map/while/body/eval_jaxpr/gpf,fd->gpd/dot_general | solution.py:51
  274.1 4.4 collective-permute-start
  278.5 15.9 %collective-permute-done = f32[1,197,1024]{2,0,1:T(1,128)S(1)} collective-permute-done((f32[1,197,1024]{2,0,1:T(1,128)S(1)}, f32[1,197,1024]{2,0,1:T(1,128)S(1)}, u32[]{:S(2)}, u32[]{:S(2)}) %collective-permute-start) | collective-permute-done | bytes 806944 | tf_op jit(solution)/shard_map/while/body/eval_jaxpr/ppermute | solution.py:15
  295.5 2.1 multiply_reduce_fusion.13
  301.6 5.6 %convolution_convert_fusion.3 = bf16[197,3072]{1,0:T(8,128)(2,1)} fusion(bf16[1024,3072]{1,0:T(8,128)(2,1)} %get-tuple-element.539, f32[1024]{0:T(1024)} %bitcast.303, f32[197]{0:T(256)S(1)} %add_rsqrt_fusion.8, f32[197]{0:T(256)S(1)} %broadcast_multiply_fusion.10, f32[1,197,1024]{2,0,1:T(1,128)S(1)} %get-tuple-element.516, ...), kind=kOutput, calls=%fused_computation.2.clone.1 | convolution fusion | flops 1241232384 | bytes 8724524 | tf_op jit(solution)/shard_map/while/body/eval_jaxpr/gpd,de->gpe/dot_general | solution.py:31
  307.2 1.6 copy.297
  309.5 2.7 fusion.341
  313.8 1.7 fusion.343
  315.8 14.2 %fusion.344 = f32[1,197,1024]{2,1,0:T(8,128)S(1)} fusion(f32[1,197,1024]{2,1,0:T(8,128)S(1)} %get-tuple-element.495, bf16[4096,1024]{1,0:T(8,128)(2,1)} %get-tuple-element.543, bf16[1024,4096]{1,0:T(8,128)(2,1)} %get-tuple-element.542, f32[1024]{0:T(1024)S(1)} %bitcast.305, f32[197]{0:T(256)S(1)} %add_rsqrt_fusion.9, ...), kind=kOutput, calls=%fused_computation.61.clone.1 | convolution fusion | flops 3358569472 | bytes 18396712 | tf_op jit(solution)/shard_map/while/body/eval_jaxpr/gpf,fd->gpd/dot_general | solution.py:51
  330.8 4.4 collective-permute-start
  335.3 14.9 %collective-permute-done = f32[1,197,1024]{2,0,1:T(1,128)S(1)} collective-permute-done((f32[1,197,1024]{2,0,1:T(1,128)S(1)}, f32[1,197,1024]{2,0,1:T(1,128)S(1)}, u32[]{:S(2)}, u32[]{:S(2)}) %collective-permute-start) | collective-permute-done | bytes 806944 | tf_op jit(solution)/shard_map/while/body/eval_jaxpr/ppermute | solution.py:15
  351.3 2.1 multiply_reduce_fusion.13
  357.4 5.6 %convolution_convert_fusion.3 = bf16[197,3072]{1,0:T(8,128)(2,1)} fusion(bf16[1024,3072]{1,0:T(8,128)(2,1)} %get-tuple-element.539, f32[1024]{0:T(1024)} %bitcast.303, f32[197]{0:T(256)S(1)} %add_rsqrt_fusion.8, f32[197]{0:T(256)S(1)} %broadcast_multiply_fusion.10, f32[1,197,1024]{2,0,1:T(1,128)S(1)} %get-tuple-element.516, ...), kind=kOutput, calls=%fused_computation.2.clone.1 | convolution fusion | flops 1241232384 | bytes 8724524 | tf_op jit(solution)/shard_map/while/body/eval_jaxpr/gpd,de->gpe/dot_general | solution.py:31
  365.3 2.7 fusion.341
  369.6 1.7 fusion.343
  371.6 14.2 %fusion.344 = f32[1,197,1024]{2,1,0:T(8,128)S(1)} fusion(f32[1,197,1024]{2,1,0:T(8,128)S(1)} %get-tuple-element.495, bf16[4096,1024]{1,0:T(8,128)(2,1)} %get-tuple-element.543, bf16[1024,4096]{1,0:T(8,128)(2,1)} %get-tuple-element.542, f32[1024]{0:T(1024)S(1)} %bitcast.305, f32[197]{0:T(256)S(1)} %add_rsqrt_fusion.9, ...), kind=kOutput, calls=%fused_computation.61.clone.1 | convolution fusion | flops 3358569472 | bytes 18396712 | tf_op jit(solution)/shard_map/while/body/eval_jaxpr/gpf,fd->gpd/dot_general | solution.py:51
  386.7 4.4 collective-permute-start
  391.1 14.0 %collective-permute-done = f32[1,197,1024]{2,0,1:T(1,128)S(1)} collective-permute-done((f32[1,197,1024]{2,0,1:T(1,128)S(1)}, f32[1,197,1024]{2,0,1:T(1,128)S(1)}, u32[]{:S(2)}, u32[]{:S(2)}) %collective-permute-start) | collective-permute-done | bytes 806944 | tf_op jit(solution)/shard_map/while/body/eval_jaxpr/ppermute | solution.py:15
  406.2 2.1 multiply_reduce_fusion.13
  410.4 3.8 convolution_convert_fusion.1
  415.6 6.1 %collective-permute-start.7 = (bf16[3,2048]{1,0:T(4,128)(2,1)S(1)}, bf16[3,2048]{1,0:T(4,128)(2,1)S(1)}, u32[]{:S(2)}, u32[]{:S(2)}) collective-permute-start(bf16[3,2048]{1,0:T(4,128)(2,1)S(1)} %slice.122), channel_id=1, source_target_pairs={{0,4},{1,5},{2,6},{3,7},{4,8},{5,9},{6,10},{7,11},{8,12},{9,13},{1... | collective-permute-start | bytes 36872 | tf_op jit(solution)/shard_map/ppermute | solution.py:15
  423.0 4.3 collective-permute-start.5
  429.0 4.5 collective-permute-start.3
  434.9 3.9 collective-permute-start.1
  445.7 8.1 %convolution_add_fusion = f32[3,1024]{1,0:T(4,128)S(1)} fusion(f32[3,1024]{1,0:T(4,128)S(1)} %get-tuple-element.399, f32[1024]{0:T(1024)S(1)} %bitcast.306, f32[3]{0:T(128)S(1)} %add_rsqrt_fusion.3, f32[3]{0:T(128)S(1)} %broadcast_multiply_fusion.4, bf16[1,4096,1024]{2,1,0:T(8,128)(2,1)} %bitcast.298, bf16[1,1024,4096]{2,1,0:T(8,128)(2,1)} %bitcast.296), kind=kOutput, calls=%fused_computation.161 | convolution fusion | flops 51145728 | bytes 16805912 | tf_op jit(solution)/shard_map/dot_general | solution.py:167
  453.7 10.4 %all_to_all.5 = f32[3,4,256]{2,0,1:T(4,128)S(1)} all-to-all(f32[3,4,256]{2,0,1:T(4,128)S(1)} %bitcast.302), channel_id=1, replica_groups=mesh['segment'=4,'lane'=32] {'segment'}, dimensions={1} | all-to-all | bytes 24576 | tf_op jit(solution)/shard_map/all_to_all | solution.py:169
  (242 shorter events, 61.8 us)
Async XLA Ops:
  6.5 65.2 %all-gather.5.cloned.1.call-start = ((), (), s32[]{:S(2)}) async-start(), calls=%async_computation.1 | async-start | bytes 8650752 | tf_op jit(solution)/shard_map/all_gather | solution.py:101
  7.3 119.4 %all-gather.7.cloned.1.call-start = ((), (), s32[]{:S(2)}) async-start(), calls=%async_computation.2 | async-start | bytes 8650752 | tf_op jit(solution)/shard_map/all_gather | solution.py:102
  140.2 1.6 copy-start
  140.7 3.1 copy-start.3
  143.8 39.3 %copy-start.2 = (f32[1024]{0:T(1024)S(1)}, f32[1024]{0:T(1024)}, u32[]{:S(2)}) copy-start(f32[1024]{0:T(1024)} %get-tuple-element.544) | copy-start | bytes 12292 | tf_op jit(solution)/shard_map/while
  158.9 21.0 %collective-permute-start = (f32[1,197,1024]{2,0,1:T(1,128)S(1)}, f32[1,197,1024]{2,0,1:T(1,128)S(1)}, u32[]{:S(2)}, u32[]{:S(2)}) collective-permute-start(f32[1,197,1024]{2,0,1:T(1,128)S(1)} %copy.298), channel_id=1, source_target_pairs={{0,32},{32,64},{64,96},{1,33},{33,65},{65,97},{2,34},{34,66},{66,9... | collective-permute-start | bytes 2420744 | tf_op jit(solution)/shard_map/while/body/eval_jaxpr/ppermute | solution.py:15
  197.7 1.6 copy-start
  198.2 3.1 copy-start.3
  201.3 39.5 %copy-start.2 = (f32[1024]{0:T(1024)S(1)}, f32[1024]{0:T(1024)}, u32[]{:S(2)}) copy-start(f32[1024]{0:T(1024)} %get-tuple-element.544) | copy-start | bytes 12292 | tf_op jit(solution)/shard_map/while
  216.4 21.2 %collective-permute-start = (f32[1,197,1024]{2,0,1:T(1,128)S(1)}, f32[1,197,1024]{2,0,1:T(1,128)S(1)}, u32[]{:S(2)}, u32[]{:S(2)}) collective-permute-start(f32[1,197,1024]{2,0,1:T(1,128)S(1)} %copy.298), channel_id=1, source_target_pairs={{0,32},{32,64},{64,96},{1,33},{33,65},{65,97},{2,34},{34,66},{66,9... | collective-permute-start | bytes 2420744 | tf_op jit(solution)/shard_map/while/body/eval_jaxpr/ppermute | solution.py:15
  255.4 1.6 copy-start
  255.9 3.1 copy-start.3
  259.0 38.6 %copy-start.2 = (f32[1024]{0:T(1024)S(1)}, f32[1024]{0:T(1024)}, u32[]{:S(2)}) copy-start(f32[1024]{0:T(1024)} %get-tuple-element.544) | copy-start | bytes 12292 | tf_op jit(solution)/shard_map/while
  274.1 20.3 %collective-permute-start = (f32[1,197,1024]{2,0,1:T(1,128)S(1)}, f32[1,197,1024]{2,0,1:T(1,128)S(1)}, u32[]{:S(2)}, u32[]{:S(2)}) collective-permute-start(f32[1,197,1024]{2,0,1:T(1,128)S(1)} %copy.298), channel_id=1, source_target_pairs={{0,32},{32,64},{64,96},{1,33},{33,65},{65,97},{2,34},{34,66},{66,9... | collective-permute-start | bytes 2420744 | tf_op jit(solution)/shard_map/while/body/eval_jaxpr/ppermute | solution.py:15
  312.2 1.6 copy-start
  312.6 3.1 copy-start.3
  315.8 37.7 %copy-start.2 = (f32[1024]{0:T(1024)S(1)}, f32[1024]{0:T(1024)}, u32[]{:S(2)}) copy-start(f32[1024]{0:T(1024)} %get-tuple-element.544) | copy-start | bytes 12292 | tf_op jit(solution)/shard_map/while
  330.8 19.4 %collective-permute-start = (f32[1,197,1024]{2,0,1:T(1,128)S(1)}, f32[1,197,1024]{2,0,1:T(1,128)S(1)}, u32[]{:S(2)}, u32[]{:S(2)}) collective-permute-start(f32[1,197,1024]{2,0,1:T(1,128)S(1)} %copy.298), channel_id=1, source_target_pairs={{0,32},{32,64},{64,96},{1,33},{33,65},{65,97},{2,34},{34,66},{66,9... | collective-permute-start | bytes 2420744 | tf_op jit(solution)/shard_map/while/body/eval_jaxpr/ppermute | solution.py:15
  368.0 1.6 copy-start
  368.5 3.1 copy-start.3
  371.6 36.7 %copy-start.2 = (f32[1024]{0:T(1024)S(1)}, f32[1024]{0:T(1024)}, u32[]{:S(2)}) copy-start(f32[1024]{0:T(1024)} %get-tuple-element.544) | copy-start | bytes 12292 | tf_op jit(solution)/shard_map/while
  386.7 18.5 %collective-permute-start = (f32[1,197,1024]{2,0,1:T(1,128)S(1)}, f32[1,197,1024]{2,0,1:T(1,128)S(1)}, u32[]{:S(2)}, u32[]{:S(2)}) collective-permute-start(f32[1,197,1024]{2,0,1:T(1,128)S(1)} %copy.298), channel_id=1, source_target_pairs={{0,32},{32,64},{64,96},{1,33},{33,65},{65,97},{2,34},{34,66},{66,9... | collective-permute-start | bytes 2420744 | tf_op jit(solution)/shard_map/while/body/eval_jaxpr/ppermute | solution.py:15
  410.0 18.8 %copy-start.13 = (pred[3,3]{0,1:T(4,128)(4,1)S(1)}, pred[3,3]{0,1:T(4,128)(4,1)}, u32[]{:S(2)}) copy-start(pred[3,3]{0,1:T(4,128)(4,1)} %get-tuple-element.379) | copy-start | bytes 31
  410.3 30.1 %copy-start.5 = (pred[3,3]{0,1:T(4,128)(4,1)S(1)}, pred[3,3]{0,1:T(4,128)(4,1)}, u32[]{:S(2)}) copy-start(pred[3,3]{0,1:T(4,128)(4,1)} %get-tuple-element.377) | copy-start | bytes 31
  410.3 30.3 %copy-start.6 = (pred[3,3]{0,1:T(4,128)(4,1)S(1)}, pred[3,3]{0,1:T(4,128)(4,1)}, u32[]{:S(2)}) copy-start(pred[3,3]{0,1:T(4,128)(4,1)} %get-tuple-element.376) | copy-start | bytes 31
  410.3 30.5 %copy-start.7 = (pred[3,3]{0,1:T(4,128)(4,1)S(1)}, pred[3,3]{0,1:T(4,128)(4,1)}, u32[]{:S(2)}) copy-start(pred[3,3]{0,1:T(4,128)(4,1)} %get-tuple-element.375) | copy-start | bytes 31
  410.3 30.6 %copy-start.8 = (pred[3,3]{0,1:T(4,128)(4,1)S(1)}, pred[3,3]{0,1:T(4,128)(4,1)}, u32[]{:S(2)}) copy-start(pred[3,3]{0,1:T(4,128)(4,1)} %get-tuple-element.374) | copy-start | bytes 31
  410.4 30.8 %copy-start.9 = (pred[3,3]{0,1:T(4,128)(4,1)S(1)}, pred[3,3]{0,1:T(4,128)(4,1)}, u32[]{:S(2)}) copy-start(pred[3,3]{0,1:T(4,128)(4,1)} %get-tuple-element.373) | copy-start | bytes 31
  410.4 31.0 %copy-start.10 = (pred[3,3]{0,1:T(4,128)(4,1)S(1)}, pred[3,3]{0,1:T(4,128)(4,1)}, u32[]{:S(2)}) copy-start(pred[3,3]{0,1:T(4,128)(4,1)} %get-tuple-element.372) | copy-start | bytes 31
  410.4 31.1 %copy-start.11 = (pred[3,3]{0,1:T(4,128)(4,1)S(1)}, pred[3,3]{0,1:T(4,128)(4,1)}, u32[]{:S(2)}) copy-start(pred[3,3]{0,1:T(4,128)(4,1)} %get-tuple-element.371) | copy-start | bytes 31
  410.4 31.3 %copy-start.12 = (pred[3,3]{0,1:T(4,128)(4,1)S(1)}, pred[3,3]{0,1:T(4,128)(4,1)}, u32[]{:S(2)}) copy-start(pred[3,3]{0,1:T(4,128)(4,1)} %get-tuple-element.378) | copy-start | bytes 31
  414.2 30.8 %copy-start.1 = (bf16[1024,1024]{1,0:T(8,128)(2,1)S(1)}, bf16[1024,1024]{1,0:T(8,128)(2,1)}, u32[]{:S(2)}) copy-start(bf16[1024,1024]{1,0:T(8,128)(2,1)} %get-tuple-element.554) | copy-start | bytes 6291460
  414.2 14.8 %collective-permute-start.8 = (bf16[3,2048]{1,0:T(4,128)(2,1)S(1)}, bf16[3,2048]{1,0:T(4,128)(2,1)S(1)}, u32[]{:S(2)}, u32[]{:S(2)}) collective-permute-start(bf16[3,2048]{1,0:T(4,128)(2,1)S(1)} %slice.122), channel_id=1, source_target_pairs={{4,0},{5,1},{6,2},{7,3},{8,4},{9,5},{10,6},{11,7},{12,8},{13,9},{1... | collective-permute-start | bytes 36872 | tf_op jit(solution)/shard_map/ppermute | solution.py:15
  415.6 17.9 %collective-permute-start.7 = (bf16[3,2048]{1,0:T(4,128)(2,1)S(1)}, bf16[3,2048]{1,0:T(4,128)(2,1)S(1)}, u32[]{:S(2)}, u32[]{:S(2)}) collective-permute-start(bf16[3,2048]{1,0:T(4,128)(2,1)S(1)} %slice.122), channel_id=1, source_target_pairs={{0,4},{1,5},{2,6},{3,7},{4,8},{5,9},{6,10},{7,11},{8,12},{9,13},{1... | collective-permute-start | bytes 36872 | tf_op jit(solution)/shard_map/ppermute | solution.py:15
  421.7 13.2 %collective-permute-start.6 = (bf16[3,2048]{1,0:T(4,128)(2,1)S(1)}, bf16[3,2048]{1,0:T(4,128)(2,1)S(1)}, u32[]{:S(2)}, u32[]{:S(2)}) collective-permute-start(bf16[3,2048]{1,0:T(4,128)(2,1)S(1)} %slice.122), channel_id=1, source_target_pairs={{3,0},{4,1},{5,2},{6,3},{7,4},{8,5},{9,6},{10,7},{11,8},{12,9},{13... | collective-permute-start | bytes 36872 | tf_op jit(solution)/shard_map/ppermute | solution.py:15
  423.0 15.9 %collective-permute-start.5 = (bf16[3,2048]{1,0:T(4,128)(2,1)S(1)}, bf16[3,2048]{1,0:T(4,128)(2,1)S(1)}, u32[]{:S(2)}, u32[]{:S(2)}) collective-permute-start(bf16[3,2048]{1,0:T(4,128)(2,1)S(1)} %slice.122), channel_id=1, source_target_pairs={{0,3},{1,4},{2,5},{3,6},{4,7},{5,8},{6,9},{7,10},{8,11},{9,12},{10... | collective-permute-start | bytes 36872 | tf_op jit(solution)/shard_map/ppermute | solution.py:15
  427.3 11.6 %collective-permute-start.4 = (bf16[3,2048]{1,0:T(4,128)(2,1)S(1)}, bf16[3,2048]{1,0:T(4,128)(2,1)S(1)}, u32[]{:S(2)}, u32[]{:S(2)}) collective-permute-start(bf16[3,2048]{1,0:T(4,128)(2,1)S(1)} %slice.122), channel_id=1, source_target_pairs={{2,0},{3,1},{4,2},{5,3},{6,4},{7,5},{8,6},{9,7},{10,8},{11,9},{12,... | collective-permute-start | bytes 36872 | tf_op jit(solution)/shard_map/ppermute | solution.py:15
  429.0 9.9 %collective-permute-start.3 = (bf16[3,2048]{1,0:T(4,128)(2,1)S(1)}, bf16[3,2048]{1,0:T(4,128)(2,1)S(1)}, u32[]{:S(2)}, u32[]{:S(2)}) collective-permute-start(bf16[3,2048]{1,0:T(4,128)(2,1)S(1)} %slice.122), channel_id=1, source_target_pairs={{0,2},{1,3},{2,4},{3,5},{4,6},{5,7},{6,8},{7,9},{8,10},{9,11},{10,... | collective-permute-start | bytes 36872 | tf_op jit(solution)/shard_map/ppermute | solution.py:15
  433.6 5.4 %collective-permute-start.2 = (bf16[3,2048]{1,0:T(4,128)(2,1)S(1)}, bf16[3,2048]{1,0:T(4,128)(2,1)S(1)}, u32[]{:S(2)}, u32[]{:S(2)}) collective-permute-start(bf16[3,2048]{1,0:T(4,128)(2,1)S(1)} %slice.122), channel_id=1, source_target_pairs={{1,0},{2,1},{3,2},{4,3},{5,4},{6,5},{7,6},{8,7},{9,8},{10,9},{11,1... | collective-permute-start | bytes 36872 | tf_op jit(solution)/shard_map/ppermute | solution.py:15
  434.9 4.7 %collective-permute-start.1 = (bf16[3,2048]{1,0:T(4,128)(2,1)S(1)}, bf16[3,2048]{1,0:T(4,128)(2,1)S(1)}, u32[]{:S(2)}, u32[]{:S(2)}) collective-permute-start(bf16[3,2048]{1,0:T(4,128)(2,1)S(1)} %slice.122), channel_id=1, source_target_pairs={{0,1},{1,2},{2,3},{3,4},{4,5},{5,6},{6,7},{7,8},{8,9},{9,10},{10,1... | collective-permute-start | bytes 36872 | tf_op jit(solution)/shard_map/ppermute | solution.py:15
  440.1 5.5 %copy-start.4 = (f32[1,1024]{1,0:T(1,128)S(1)}, f32[1,1024]{1,0:T(1,128)}, u32[]{:S(2)}) copy-start(f32[1,1024]{1,0:T(1,128)} %get-tuple-element.582) | copy-start | bytes 12292
Sparse Core Ops, SparseCore 0:
  9.5 62.1 all-gather.4
  74.0 52.6 all-gather.6
where the time goes:
time: 480 us; the launch traced here: 472 us
  waiting for transfers between devices  197 us (41%)
  matrix products  129 us (27%)
  other arithmetic  52.1 us (11%)
  starting transfers between devices  45.3 us (9%)
  local copies, waits for them, and re-layouts  22 us (5%)
  between operations  14.1 us (3%)
  blocking collectives  10.4 us (2%)
    ppermute x13, waiting for transfers between devices, from_behind(): lax.ppermute(value, axis, [(source, source + steps) for source in range(l...  79.2 us
    dot_general x5, matrix products, spatial_layer(): jnp.einsum('gpf,fd->gpd', hidden, reduce_weight, preferred_element_type=j...  71.1 us
    all_gather x1, waiting for transfers between devices, body(): lax.all_gather(expand_weight[0], 'lane', axis=1, tiled=True)  61.6 us
    all_gather x1, waiting for transfers between devices, body(): lax.all_gather(reduce_weight[0], 'lane', axis=0, tiled=True)  54.9 us
    ppermute x13, starting transfers between devices, from_behind(): lax.ppermute(value, axis, [(source, source + steps) for source in range(l...  45.3 us
    dot_general x5, matrix products, spatial_layer(): jnp.einsum('gpd,de->gpe', normed, triple_weight, preferred_element_type=j...  28 us
    reduce_sum x17, other arithmetic, normalize(): spread = jnp.mean(centred * centred, axis=-1, keepdims=True)  18.5 us
    sub x5, other arithmetic, spatial_layer(): weights = jax.nn.softmax(scores, axis=-1).astype(jnp.bfloat16)  13.5 us
  transfers between devices with their start and end apart: 15, of which 8 were waited for; matrix products, arithmetic and copies ran while one was open for 1% of the time, Pallas kernels for 0%

commit v1 on v0

v1 whole, which is shorter than its diff:
```python
import functools
import math

import jax
import jax.numpy as jnp
from jax import lax
from jax.experimental import pallas as pl
from jax.experimental.pallas import tpu as pltpu
from jax.sharding import PartitionSpec as P

HEADS = 16
ROWS = 197
PAD = 208
D = 1024
FF = 4096
NF = 3
REACH = 4
SLOTS = 2 * REACH + 1
KEYS = 80
MESH = pl.DeviceIdType.MESH
F32 = jnp.float32
BF = jnp.bfloat16


def dot(a, b):
    return lax.dot_general(a, b, (((1,), (0,)), ((), ())), preferred_element_type=F32)


def dot_t(a, b):
    return lax.dot_general(a, b, (((1,), (1,)), ((), ())), preferred_element_type=F32)


def gelu(x):
    return 0.5 * x * (1.0 + lax.erf(x * (1.0 / math.sqrt(2.0))))


def norm_rows(x, gain):
    average = jnp.mean(x, axis=-1, keepdims=True)
    centred = x - average
    spread = jnp.mean(centred * centred, axis=-1, keepdims=True)
    return centred * lax.rsqrt(spread + 1e-06) * gain


def kernel(
    frames_ref, triple_hbm, output_hbm, expand_hbm, reduce_hbm, again_ref, dgain_ref, fgain_ref, shot_ref,
    out_ref,
    exp_v, red_v, trip_v, outw_v, state, inb, outb, packed, act, ctx, pooled, pin, obuf, rbuf,
    local_sem, send_sem, recv_sem, sib_send, sib_recv, rel_send, rel_recv, pool_send, pool_recv, fin_send, fin_recv,
):
    seg = lax.axis_index("segment")
    lane = lax.axis_index("lane")
    cx = lane // 8
    cz = (lane // 2) % 4
    core = lane % 2

    def lane_at(x, z, c):
        return ((x % 4) * 4 + (z % 4)) * 2 + c

    loads = [
        pltpu.make_async_copy(triple_hbm.at[0], trip_v, local_sem.at[0]),
        pltpu.make_async_copy(output_hbm.at[0], outw_v, local_sem.at[1]),
    ]
    for copy in loads:
        copy.start()

    peers = [
        (seg, lane_at(cx + 1, cz, core)), (seg, lane_at(cx + 3, cz, core)),
        (seg, lane_at(cx, cz + 1, core)), (seg, lane_at(cx, cz + 3, core)),
        (seg, lane_at(cx, cz, 1 - core)), ((seg + 2) % 4, lane),
    ]
    for d in range(-REACH, REACH + 1):
        peers.append(((seg + 1) % 4, (lane + d + 32) % 32))
        peers.append(((seg + 3) % 4, (lane - d + 32) % 32))
    barrier = pltpu.get_barrier_semaphore()
    for peer in peers:
        pl.semaphore_signal(barrier, inc=1, device_id=peer, device_id_type=MESH)
    pl.semaphore_wait(barrier, len(peers))

    def shard_lane(kind, dp, dq, c):
        if kind == 0:
            return lane_at(cx + dp + 4, cz + dq + 4, c)
        return lane_at(cx + dq + 4, cz + dp + 4, c)

    def region(kind, owner, half):
        if kind == 0:
            cols = pl.ds(pl.multiple_of(owner * 128, 128), 128)
            rows = pl.ds(0, D) if half is None else pl.ds(half * (D // 2), D // 2)
            return exp_v.at[rows, cols]
        if half is None:
            return red_v.at[pl.ds(pl.multiple_of(owner * 128, 128), 128), :]
        return red_v.at[pl.ds(pl.multiple_of(owner * 128 + half * 64, 64), 64), :]

    own_src = (expand_hbm.at[0], reduce_hbm.at[0])

    def neighbour(kind, along_p, sign):
        s = sign + 4
        if (kind == 0) == along_p:
            return (seg, lane_at(cx + s, cz, core))
        return (seg, lane_at(cx, cz + s, core))

    def hop(kind, dp, dq, half, along_p, sign):
        rp, rq = (dp - sign, dq) if along_p else (dp, dq - sign)
        h = half or 0
        dst = region(kind, shard_lane(kind, dp, dq, core), half)
        own = dp == 0 and dq == 0
        return pltpu.make_async_remote_copy(
            src_ref=own_src[kind] if own else dst, dst_ref=dst,
            send_sem=send_sem.at[kind, rp % 4, rq % 4, h], recv_sem=recv_sem.at[kind, rp % 4, rq % 4, h],
            device_id=neighbour(kind, along_p, sign), device_id_type=MESH)

    def arrival(kind, rp, rq, half):
        h = half or 0
        dst = region(kind, shard_lane(kind, rp, rq, core), half)
        return pltpu.make_async_remote_copy(
            src_ref=dst, dst_ref=dst,
            send_sem=send_sem.at[kind, rp % 4, rq % 4, h], recv_sem=recv_sem.at[kind, rp % 4, rq % 4, h],
            device_id=neighbour(kind, True, 1), device_id_type=MESH)

    def sibling(kind, dp, dq, receive=False):
        c = 1 - core if receive else core
        dst = region(kind, shard_lane(kind, dp, dq, c), None)
        own = dp == 0 and dq == 0 and not receive
        return pltpu.make_async_remote_copy(
            src_ref=own_src[kind] if own else dst, dst_ref=dst,
            send_sem=sib_send.at[kind, dp % 4, dq % 4], recv_sem=sib_recv.at[kind, dp % 4, dq % 4],
            device_id=(seg, lane_at(cx, cz, 1 - core)), device_id_type=MESH)

    sent = []

    def go(copy):
        copy.start()
        sent.append(copy)

    for kind in range(2):
        for sign in (1, -1):
            go(hop(kind, 0, 0, None, True, sign))
    for kind in range(2):
        for sign in (1, -1):
            go(hop(kind, 0, 0, None, False, sign))
        go(sibling(kind, 0, 0))
        mine = pltpu.make_async_copy(own_src[kind], region(kind, lane, None), local_sem.at[2 + kind])
        mine.start()
        loads.append(mine)

    def spread(kind, dp):
        for sign in (1, -1):
            go(hop(kind, dp, 0, None, False, sign))
        go(sibling(kind, dp, 0))

    def ev_p(kind, rp):
        arrival(kind, rp, 0, None).wait_recv()
        go(hop(kind, rp, 0, 0 if rp < 0 else 1, True, -rp))
        spread(kind, rp)

    def ev_p2(kind):
        arrival(kind, 2, 0, 0).wait_recv()
        arrival(kind, 2, 0, 1).wait_recv()
        spread(kind, 2)

    def ev_q(kind, rp, rq):
        arrival(kind, rp, rq, None).wait_recv()
        go(hop(kind, rp, rq, 0 if rq < 0 else 1, False, -rq))
        go(sibling(kind, rp, rq))

    def ev_q2(kind, rp):
        arrival(kind, rp, 2, 0).wait_recv()
        arrival(kind, rp, 2, 1).wait_recv()
        go(sibling(kind, rp, 2))

    events = []

    def both(fn, *args):
        for kind in range(2):
            events.append(functools.partial(fn, kind, *args))

    both(ev_p, -1)
    both(ev_p, 1)
    both(ev_q, 0, -1)
    both(ev_q, 0, 1)
    both(ev_p2)
    both(ev_q, -1, -1)
    both(ev_q, -1, 1)
    both(ev_q, 1, -1)
    both(ev_q, 1, 1)
    both(ev_q2, 0)
    both(ev_q, 2, -1)
    both(ev_q, 2, 1)
    both(ev_q2, -1)
    both(ev_q2, 1)
    both(ev_q2, 2)

    def norm_into(f, gain_ref):
        gain = gain_ref[...]
        for i in range(PAD // 16):
            rows = pl.ds(16 * i, 16)
            act[rows, :] = norm_rows(state[f, rows, :], gain).astype(BF)

    def project(f):
        norm_into(f, again_ref)

        def chunk(n, carry):
            cols = pl.ds(pl.multiple_of(n * 512, 512), 512)
            packed[:, cols] = dot(act[...], trip_v[:, cols]).astype(BF)
            return carry

        lax.fori_loop(0, 6, chunk, 0)

    def attend():
        low = lax.broadcasted_iota(jnp.int32, (PAD, 128), 1) < 64
        bias = jnp.where(lax.broadcasted_iota(jnp.int32, (1, PAD), 1) < ROWS, 0.0, -1e30).astype(F32)

        def pair(j, carry):
            at = pl.multiple_of(j * 128, 128)
            q = packed[:, pl.ds(at, 128)]
            k = packed[:, pl.ds(pl.multiple_of(at + D, 128), 128)]
            v = packed[:, pl.ds(pl.multiple_of(at + 2 * D, 128), 128)]
            parts = []
            for keep in (low, ~low):
                scores = dot_t(jnp.where(keep, q * 0.125, 0.0).astype(BF), k) + bias
                shares = jnp.exp(scores - jnp.max(scores, axis=-1, keepdims=True))
                total = jnp.sum(shares, axis=-1, keepdims=True)
                parts.append(dot(shares.astype(BF), v) / total)
            ctx[:, pl.ds(at, 128)] = jnp.where(low, parts[0], parts[1]).astype(BF)
            return carry

        lax.fori_loop(0, 8, pair, 0)

    def join(f):
        def chunk(n, carry):
            cols = pl.ds(pl.multiple_of(n * 512, 512), 512)
            state[f, :, cols] += dot(ctx[...], outw_v[:, cols])
            return carry

        lax.fori_loop(0, 2, chunk, 0)

    def feed(f):
        norm_into(f, dgain_ref)

        def chunk(n, carry):
            part = pl.ds(pl.multiple_of(n * 512, 512), 512)
            hidden = gelu(dot(act[...], exp_v[:, part])).astype(BF)
            state[f] += dot(hidden, red_v[part, :])
            return carry

        lax.fori_loop(0, 8, chunk, 0)

    for copy in loads[:2]:
        copy.wait()

    todo = list(events)

    def pump(count):
        for _ in range(min(count, len(todo))):
            todo.pop(0)()

    for f in range(NF):
        @pl.when(seg == 0)
        def _():
            state[f, 192:PAD, :] = jnp.zeros((PAD - 192, D), F32)
            state[f, 0:ROWS, :] = frames_ref[f].astype(F32)
            project(f)

        pump(4)

        @pl.when(seg == 0)
        def _():
            attend()

        pump(3)

        @pl.when(seg == 0)
        def _():
            join(f)

        pump(2)
    pump(len(todo))
    for kind in range(2):
        for dp in range(4):
            for dq in range(4):
                sibling(kind, dp, dq, receive=True).wait_recv()
    for copy in loads[2:]:
        copy.wait()

    def relay(f):
        return pltpu.make_async_remote_copy(
            src_ref=outb.at[f], dst_ref=inb.at[f], send_sem=rel_send.at[f], recv_sem=rel_recv.at[f],
            device_id=((seg + 1) % 4, lane), device_id_type=MESH)

    @pl.when(seg == 2)
    def _():
        pooled[...] = jnp.zeros_like(pooled)

    @pl.when(seg < 3)
    def _():
        def step(f, carry):
            @pl.when(seg > 0)
            def _():
                relay(f).wait_recv()
                state[f] = inb[f].astype(F32)
                project(f)
                attend()
                join(f)

            feed(f)

            @pl.when(seg < 2)
            def _():
                outb[f] = state[f].astype(BF)
                relay(f).start()

            @pl.when(seg == 2)
            def _():
                gain = fgain_ref[...]
                total = jnp.zeros((16, D), F32)
                for i in range(PAD // 16):
                    rows = norm_rows(state[f, pl.ds(16 * i, 16), :], gain)
                    if 16 * i + 16 > ROWS:
                        keep = lax.broadcasted_iota(jnp.int32, (16, D), 0) < ROWS - 16 * i
                        rows = jnp.where(keep, rows, 0.0)
                    total = total + rows
                pooled[pl.ds(f, 1), :] = jnp.sum(total, axis=0, keepdims=True) * (1.0 / ROWS)

            return carry

        lax.fori_loop(0, NF, step, 0)

    def pool_copy(d):
        return pltpu.make_async_remote_copy(
            src_ref=pooled, dst_ref=pin.at[pl.ds(8 * (d + REACH), 8), :],
            send_sem=pool_send.at[d + REACH], recv_sem=pool_recv.at[d + REACH],
            device_id=((seg + 1) % 4, (lane - d + 32) % 32), device_id_type=MESH)

    def result_copy(section):
        return pltpu.make_async_remote_copy(
            src_ref=obuf.at[section], dst_ref=rbuf, send_sem=fin_send.at[section], recv_sem=fin_recv,
            device_id=(section, lane), device_id_type=MESH)

    @pl.when(seg == 2)
    def _():
        for d in range(-REACH, REACH + 1):
            pool_copy(d).start()

    @pl.when(seg == 3)
    def _():
        pin[8 * SLOTS:KEYS, :] = jnp.zeros((KEYS - 8 * SLOTS, D), F32)
        for d in range(-REACH, REACH + 1):
            pool_copy(d).wait_recv()
        again = again_ref[...]
        for i in range(KEYS // 16):
            rows = pl.ds(16 * i, 16)
            act[rows, :] = norm_rows(pin[rows, :], again).astype(BF)

        def chunk(n, carry):
            cols = pl.ds(pl.multiple_of(n * 512, 512), 512)
            packed[0:KEYS, cols] = dot(act[0:KEYS, :], trip_v[:, cols]).astype(BF)
            return carry

        lax.fori_loop(0, 6, chunk, 0)

        col = lax.broadcasted_iota(jnp.int32, (16, KEYS), 1)
        row = lax.broadcasted_iota(jnp.int32, (16, KEYS), 0)
        key_lane = (lane + (col >> 3) - REACH + 32) & 31
        key_at = key_lane * NF + (col & 7)
        own_at = lane * NF + jnp.minimum(row, NF - 1)
        key_shot = jnp.zeros((16, KEYS), jnp.int32)
        own_shot = jnp.zeros((16, KEYS), jnp.int32)
        end = 0
        for s in range(24):
            end = end + shot_ref[s]
            key_shot += (key_at >= end).astype(jnp.int32)
            own_shot += (own_at >= end).astype(jnp.int32)
        allowed = (key_shot == own_shot) & ((col & 7) < NF) & (col < 8 * SLOTS)
        low = lax.broadcasted_iota(jnp.int32, (16, 128), 1) < 64
        mine = 8 * REACH

        def pair(j, carry):
            at = pl.multiple_of(j * 128, 128)
            q = packed[mine:mine + 16, pl.ds(at, 128)]
            k = packed[0:KEYS, pl.ds(pl.multiple_of(at + D, 128), 128)]
            v = packed[0:KEYS, pl.ds(pl.multiple_of(at + 2 * D, 128), 128)]
            parts = []
            for keep in (low, ~low):
                scores = dot_t(jnp.where(keep, q * 0.125, 0.0).astype(BF), k)
                scores = jnp.where(allowed, scores, -1e30)
                shares = jnp.exp(scores - jnp.max(scores, axis=-1, keepdims=True))
                total = jnp.sum(shares, axis=-1, keepdims=True)
                high = shares.astype(BF)
                rest = (shares - high.astype(F32)).astype(BF)
                parts.append((dot(high, v) + dot(rest, v)) / total)
            ctx[0:16, pl.ds(at, 128)] = jnp.where(low, parts[0], parts[1]).astype(BF)
            return carry

        lax.fori_loop(0, 8, pair, 0)
        temporal = pin[mine:mine + 16, :] + dot(ctx[0:16, :], outw_v[...])
        state[0, 0:16, :] = temporal
        act[0:16, :] = norm_rows(temporal, dgain_ref[...]).astype(BF)

        def ff_chunk(n, carry):
            part = pl.ds(pl.multiple_of(n * 512, 512), 512)
            hidden = gelu(dot(act[0:16, :], exp_v[:, part])).astype(BF)
            state[0, 0:16, :] += dot(hidden, red_v[part, :])
            return carry

        lax.fori_loop(0, 8, ff_chunk, 0)
        for section in range(4):
            obuf[section] = state[0, 0:8, 256 * section:256 * section + 256]
        for section in range(3):
            result_copy(section).start()
        out_ref[...] = obuf[3, 0:NF, :]
        for section in range(3):
            result_copy(section).wait_send()

    @pl.when(seg == 2)
    def _():
        for d in range(-REACH, REACH + 1):
            pool_copy(d).wait_send()

    @pl.when(seg < 2)
    def _():
        for f in range(NF):
            relay(f).wait_send()

    for copy in sent:
        copy.wait_send()

    @pl.when(seg < 3)
    def _():
        result_copy(0).wait_recv()
        out_ref[...] = rbuf[0:NF, :]


def body(frames, triple_weight, output_weight, expand_weight, reduce_weight, attend_gain, dense_gain, final_gain, shot_lengths):
    vmem = pl.BlockSpec(memory_space=pltpu.VMEM)
    anywhere = pl.BlockSpec(memory_space=pl.ANY)
    dma = pltpu.SemaphoreType.DMA
    return pl.pallas_call(
        kernel,
        out_shape=jax.ShapeDtypeStruct((NF, 256), F32),
        in_specs=[vmem, anywhere, anywhere, anywhere, anywhere, vmem, vmem, vmem,
                  pl.BlockSpec(memory_space=pltpu.SMEM)],
        out_specs=vmem,
        scratch_shapes=[
            pltpu.VMEM((D, FF), BF), pltpu.VMEM((FF, D), BF), pltpu.VMEM((D, 3 * D), BF), pltpu.VMEM((D, D), BF),
            pltpu.VMEM((NF, PAD, D), F32), pltpu.VMEM((NF, PAD, D), BF), pltpu.VMEM((NF, PAD, D), BF),
            pltpu.VMEM((PAD, 3 * D), BF), pltpu.VMEM((PAD, D), BF), pltpu.VMEM((PAD, D), BF),
            pltpu.VMEM((8, D), F32), pltpu.VMEM((KEYS, D), F32), pltpu.VMEM((4, 8, 256), F32), pltpu.VMEM((8, 256), F32),
            dma((4,)), dma((2, 4, 4, 2)), dma((2, 4, 4, 2)), dma((2, 4, 4)), dma((2, 4, 4)),
            dma((NF,)), dma((NF,)), dma((SLOTS,)), dma((SLOTS,)), dma((3,)), dma(()),
        ],
        compiler_params=pltpu.CompilerParams(
            collective_id=0, has_side_effects=True, vmem_limit_bytes=60 * 1024 * 1024),
    )(frames, triple_weight, output_weight, expand_weight, reduce_weight, attend_gain, dense_gain,
      final_gain.reshape(1, D), shot_lengths)


def solution(mesh):
    return jax.shard_map(
        body,
        mesh=mesh,
        in_specs=(
            P("lane", None, None),
            P("segment", None, None),
            P("segment", None, None),
            P("segment", None, "lane"),
            P("segment", "lane", None),
            P("segment", None),
            P("segment", None),
            P(),
            P(),
        ),
        out_specs=P("lane", "segment"),
        check_vma=False,
    )
```

time: 480 us -> 174 us (0.36); the launches traced: 472 us -> 173 us
  waiting for transfers between devices: 197 us -> 0 us
  Pallas kernels: 0 us -> 172 us
  matrix products: 129 us -> 0 us
  other arithmetic: 52.1 us -> 0 us
  starting transfers between devices: 45.3 us -> 0 us
  local copies, waits for them, and re-layouts: 22 us -> 1.28 us
  between operations: 14.1 us -> 0.01 us
  blocking collectives: 10.4 us -> 0 us
    pallas_call x0 -> x1, Pallas kernels: none -> 172 us  [body(): pl.pallas_call(kernel, out_shape=jax.ShapeDtypeStruct((NF, 256), F32), in...]
    dot_general x46 -> x0, matrix products: 129 us -> none  [the longest x5 71.1 us: spatial_layer(): jnp.einsum('gpf,fd->gpd', hidden, reduce_weight, preferred_element_type=j...]
    all_gather x2 -> x0, waiting for transfers between devices: 117 us -> none  [the longest x1 61.6 us: body(): lax.all_gather(expand_weight[0], 'lane', axis=1, tiled=True)]
    ppermute x13 -> x0, waiting for transfers between devices: 79.2 us -> none  [from_behind(): lax.ppermute(value, axis, [(source, source + steps) for source in range(l...]
    ppermute x13 -> x0, starting transfers between devices: 45.3 us -> none  [from_behind(): lax.ppermute(value, axis, [(source, source + steps) for source in range(l...]
    reduce_sum x43 -> x0, other arithmetic: 37.3 us -> none  [the longest x17 18.5 us: normalize(): spread = jnp.mean(centred * centred, axis=-1, keepdims=True)]
    sub x5 -> x0, other arithmetic: 13.5 us -> none  [spatial_layer(): weights = jax.nn.softmax(scores, axis=-1).astype(jnp.bfloat16)]
    all_to_all x1 -> x0, blocking collectives: 10.4 us -> none  [body(): lax.all_to_all(columns, 'segment', split_axis=1, concat_axis=1, tiled=True)]
  transfers between devices with their start and end apart: 15 -> 0, of which waited for: 8 -> 0; matrix products, arithmetic and copies ran while one was open for 1% -> 0% of each run, Pallas kernels for 0% -> 0%
where the time goes in v1:
time: 174 us; the launch traced here: 173 us
  Pallas kernels  172 us (99%)
    pallas_call x1, Pallas kernels, body(): pl.pallas_call(kernel, out_shape=jax.ShapeDtypeStruct((NF, 256), F32), in...  172 us

profile of v1, /device:TPU:0, one launch (start us, length us, event | category | flops | bytes accessed | tf_op | source)
XLA Modules:
  0.0 173.4 jit_solution(11034940401817614117)
XLA Ops:
  0.0 172.1 %shard_map.91 = f32[3,256]{1,0:T(4,128)} custom-call(bf16[3,197,1024]{2,1,0:T(8,128)(2,1)} %frames_ref.1, bf16[1,1024,3072]{2,1,0:T(8,128)(2,1)} %triple_hbm.1, bf16[1,1024,1024]{2,1,0:T(8,128)(2,1)} %output_hbm.1, bf16[1,1024,128]{2,1,0:T(8,128)(2,1)} %expand_hbm.1, bf16[1,128,1024]{2,1,0:T(8,128)(2,1)} %reduce_hbm.1, f32[1,1024]{1,0:T(1,128)} %again_ref.1, ...), custom_call_target="tpu_custom_call" | custom-call | tf_op jit(solution)/shard_map/pallas_call | solution.py:436
  172.1 1.3 copy.11

commit v2 on v1

--- a/solution.py
+++ b/solution.py
@@ -198,51 +198,37 @@
     def project(f):
         norm_into(f, again_ref)
 
-        def chunk(n, carry):
-            cols = pl.ds(pl.multiple_of(n * 512, 512), 512)
-            packed[:, cols] = dot(act[...], trip_v[:, cols]).astype(BF)
-            return carry
-
-        lax.fori_loop(0, 6, chunk, 0)
+        for at in range(0, 3 * D, 256):
+            packed[:, at:at + 256] = dot(act[...], trip_v[:, at:at + 256]).astype(BF)
 
     def attend():
         low = lax.broadcasted_iota(jnp.int32, (PAD, 128), 1) < 64
         bias = jnp.where(lax.broadcasted_iota(jnp.int32, (1, PAD), 1) < ROWS, 0.0, -1e30).astype(F32)
 
-        def pair(j, carry):
-            at = pl.multiple_of(j * 128, 128)
-            q = packed[:, pl.ds(at, 128)]
-            k = packed[:, pl.ds(pl.multiple_of(at + D, 128), 128)]
-            v = packed[:, pl.ds(pl.multiple_of(at + 2 * D, 128), 128)]
+        for at in range(0, D, 128):
+            q = packed[:, at:at + 128]
+            k = packed[:, D + at:D + at + 128]
+            v = packed[:, 2 * D + at:2 * D + at + 128]
             parts = []
             for keep in (low, ~low):
                 scores = dot_t(jnp.where(keep, q * 0.125, 0.0).astype(BF), k) + bias
                 shares = jnp.exp(scores - jnp.max(scores, axis=-1, keepdims=True))
                 total = jnp.sum(shares, axis=-1, keepdims=True)
                 parts.append(dot(shares.astype(BF), v) / total)
-            ctx[:, pl.ds(at, 128)] = jnp.where(low, parts[0], parts[1]).astype(BF)
-            return carry
-
-        lax.fori_loop(0, 8, pair, 0)
+            ctx[:, at:at + 128] = jnp.where(low, parts[0], parts[1]).astype(BF)
 
     def join(f):
-        def chunk(n, carry):
-            cols = pl.ds(pl.multiple_of(n * 512, 512), 512)
-            state[f, :, cols] += dot(ctx[...], outw_v[:, cols])
-            return carry
-
-        lax.fori_loop(0, 2, chunk, 0)
+        for at in range(0, D, 256):
+            state[f, :, at:at + 256] += dot(ctx[...], outw_v[:, at:at + 256])
 
     def feed(f):
         norm_into(f, dgain_ref)
-
-        def chunk(n, carry):
-            part = pl.ds(pl.multiple_of(n * 512, 512), 512)
-            hidden = gelu(dot(act[...], exp_v[:, part])).astype(BF)
-            state[f] += dot(hidden, red_v[part, :])
-            return carry
-
-        lax.fori_loop(0, 8, chunk, 0)
+        wide = dot(act[...], exp_v[:, 0:256])
+        for at in range(0, FF, 256):
+            hidden = gelu(wide).astype(BF)
+            if at + 256 < FF:
+                wide = dot(act[...], exp_v[:, at + 256:at + 512])
+            state[f] += dot(hidden, red_v[at:at + 256, :])
 
     for copy in loads[:2]:
         copy.wait()

time: 174 us -> 142 us (0.82)
  Pallas kernels: 172 us -> 140 us
    pallas_call x1, Pallas kernels: 172 us -> 140 us  [body(): pl.pallas_call(kernel, out_shape=jax.ShapeDtypeStruct((NF, 256), F32), in...]
where the time goes in v2:
time: 142 us; the launch traced here: 141 us
  Pallas kernels  140 us (99%)
    pallas_call x1, Pallas kernels, body(): pl.pallas_call(kernel, out_shape=jax.ShapeDtypeStruct((NF, 256), F32), in...  140 us

profile of v2, /device:TPU:0, one launch (start us, length us, event | category | flops | bytes accessed | tf_op | source)
XLA Modules:
  0.0 140.8 jit_solution(18411758544905391351)
XLA Ops:
  0.0 139.5 %shard_map.91 = f32[3,256]{1,0:T(4,128)} custom-call(bf16[3,197,1024]{2,1,0:T(8,128)(2,1)} %frames_ref.1, bf16[1,1024,3072]{2,1,0:T(8,128)(2,1)} %triple_hbm.1, bf16[1,1024,1024]{2,1,0:T(8,128)(2,1)} %output_hbm.1, bf16[1,1024,128]{2,1,0:T(8,128)(2,1)} %expand_hbm.1, bf16[1,128,1024]{2,1,0:T(8,128)(2,1)} %reduce_hbm.1, f32[1,1024]{1,0:T(1,128)} %again_ref.1, ...), custom_call_target="tpu_custom_call" | custom-call | tf_op jit(solution)/shard_map/pallas_call | solution.py:422
  139.5 1.3 copy.11

commit v3 on v2

v3 whole, which is shorter than its diff:
```python
import functools
import math

import jax
import jax.numpy as jnp
from jax import lax
from jax.experimental import pallas as pl
from jax.experimental.pallas import tpu as pltpu
from jax.sharding import PartitionSpec as P

HEADS = 16
ROWS = 197
PAD = 208
D = 1024
FF = 4096
NF = 3
REACH = 4
SLOTS = 2 * REACH + 1
KEYS = 80
MESH = pl.DeviceIdType.MESH
F32 = jnp.float32
BF = jnp.bfloat16


def dot(a, b):
    return lax.dot_general(a, b, (((1,), (0,)), ((), ())), preferred_element_type=F32)


def dot_t(a, b):
    return lax.dot_general(a, b, (((1,), (1,)), ((), ())), preferred_element_type=F32)


def gelu(x):
    return 0.5 * x * (1.0 + lax.erf(x * (1.0 / math.sqrt(2.0))))


def norm_rows(x, gain):
    average = jnp.mean(x, axis=-1, keepdims=True)
    centred = x - average
    spread = jnp.mean(centred * centred, axis=-1, keepdims=True)
    return centred * lax.rsqrt(spread + 1e-06) * gain


def kernel(
    frames_ref, triple_hbm, output_hbm, expand_hbm, reduce_hbm, again_ref, dgain_ref, fgain_ref, shot_ref,
    out_ref,
    exp_v, red_v, exp_h, red_h, trip_v, outw_v, state, inb, inp, outb, outy, packed, act, ctx, pooled, pin, obuf, rbuf,
    local_sem, send_sem, recv_sem, sib_send, sib_recv, hsend_sem, hrecv_sem, hsib_send, hsib_recv,
    rel_send, rel_recv, early_send, part_send, part_recv, shard_send, shard_recv,
    pool_send, pool_recv, fin_send, fin_recv,
):
    seg = lax.axis_index("segment")
    lane = lax.axis_index("lane")
    cx = lane // 8
    cz = (lane // 2) % 4
    core = lane % 2

    def lane_at(x, z, c):
        return ((x % 4) * 4 + (z % 4)) * 2 + c

    loads = [
        pltpu.make_async_copy(triple_hbm.at[0], trip_v, local_sem.at[0]),
        pltpu.make_async_copy(output_hbm.at[0], outw_v, local_sem.at[1]),
    ]
    for copy in loads:
        copy.start()

    peers = [
        (seg, lane_at(cx + 1, cz, core)), (seg, lane_at(cx + 3, cz, core)),
        (seg, lane_at(cx, cz + 1, core)), (seg, lane_at(cx, cz + 3, core)),
        (seg, lane_at(cx, cz, 1 - core)),
        ((seg + 1) % 4, lane), ((seg + 2) % 4, lane), ((seg + 3) % 4, lane),
    ]
    barrier = pltpu.get_barrier_semaphore()
    for peer in peers:
        pl.semaphore_signal(barrier, inc=1, device_id=peer, device_id_type=MESH)
    pl.semaphore_wait(barrier, len(peers))

    own_src = (expand_hbm.at[0], reduce_hbm.at[0])

    def pane(exp_ref, red_ref, kind, owner, half):
        if kind == 0:
            cols = pl.ds(pl.multiple_of(owner * 128, 128), 128)
            rows = pl.ds(0, D) if half is None else pl.ds(half * (D // 2), D // 2)
            return exp_ref.at[rows, cols]
        if half is None:
            return red_ref.at[pl.ds(pl.multiple_of(owner * 128, 128), 128), :]
        return red_ref.at[pl.ds(pl.multiple_of(owner * 128 + half * 64, 64), 64), :]

    def make_ring(exp_ref, red_ref, halved, ssem, rsem, bsend, brecv):
        def region(kind, dp, dq, c, half):
            x, z = (cx + dp + 4, cz + dq + 4) if kind == 0 else (cx + dq + 4, cz + dp + 4)
            owner = lane_at(x, z, 0) // 2 if halved else lane_at(x, z, c)
            return pane(exp_ref, red_ref, kind, owner, half)

        def neighbour(kind, along_p, sign):
            s = sign + 4
            if (kind == 0) == along_p:
                return (seg, lane_at(cx + s, cz, core))
            return (seg, lane_at(cx, cz + s, core))

        def source(kind, dp, dq, dst):
            return own_src[kind] if dp == 0 and dq == 0 and not halved else dst

        def hop(kind, dp, dq, half, along_p, sign):
            rp, rq = (dp - sign, dq) if along_p else (dp, dq - sign)
            h = half or 0
            dst = region(kind, dp, dq, core, half)
            return pltpu.make_async_remote_copy(
                src_ref=source(kind, dp, dq, dst), dst_ref=dst,
                send_sem=ssem.at[kind, rp % 4, rq % 4, h], recv_sem=rsem.at[kind, rp % 4, rq % 4, h],
                device_id=neighbour(kind, along_p, sign), device_id_type=MESH)

        def arrival(kind, rp, rq, half):
            h = half or 0
            dst = region(kind, rp, rq, core, half)
            return pltpu.make_async_remote_copy(
                src_ref=dst, dst_ref=dst,
                send_sem=ssem.at[kind, rp % 4, rq % 4, h], recv_sem=rsem.at[kind, rp % 4, rq % 4, h],
                device_id=neighbour(kind, True, 1), device_id_type=MESH)

        def sibling(kind, dp, dq, receive=False):
            dst = region(kind, dp, dq, 1 - core if receive else core, None)
            return pltpu.make_async_remote_copy(
                src_ref=dst if receive else source(kind, dp, dq, dst), dst_ref=dst,
                send_sem=bsend.at[kind, dp % 4, dq % 4], recv_sem=brecv.at[kind, dp % 4, dq % 4],
                device_id=(seg, lane_at(cx, cz, 1 - core)), device_id_type=MESH)

        sent = []

        def go(make, *args):
            make(*args).start()
            sent.append((make, args))

        def start():
            for kind in range(2):
                for sign in (1, -1):
                    go(hop, kind, 0, 0, None, True, sign)
            for kind in range(2):
                for sign in (1, -1):
                    go(hop, kind, 0, 0, None, False, sign)
                go(sibling, kind, 0, 0)

        def spread(kind, dp):
            for sign in (1, -1):
                go(hop, kind, dp, 0, None, False, sign)
            go(sibling, kind, dp, 0)

        def ev_p(kind, rp):
            arrival(kind, rp, 0, None).wait_recv()
            go(hop, kind, rp, 0, 0 if rp < 0 else 1, True, -rp)
            spread(kind, rp)

        def ev_p2(kind):
            arrival(kind, 2, 0, 0).wait_recv()
            arrival(kind, 2, 0, 1).wait_recv()
            spread(kind, 2)

        def ev_q(kind, rp, rq):
            arrival(kind, rp, rq, None).wait_recv()
            go(hop, kind, rp, rq, 0 if rq < 0 else 1, False, -rq)
            go(sibling, kind, rp, rq)

        def ev_q2(kind, rp):
            arrival(kind, rp, 2, 0).wait_recv()
            arrival(kind, rp, 2, 1).wait_recv()
            go(sibling, kind, rp, 2)

        events = []

        def both(fn, *args):
            for kind in range(2):
                events.append(functools.partial(fn, kind, *args))

        both(ev_p, -1)
        both(ev_p, 1)
        both(ev_q, 0, -1)
        both(ev_q, 0, 1)
        both(ev_p2)
        both(ev_q, -1, -1)
        both(ev_q, -1, 1)
        both(ev_q, 1, -1)
        both(ev_q, 1, 1)
        both(ev_q2, 0)
        both(ev_q, 2, -1)
        both(ev_q, 2, 1)
        both(ev_q2, -1)
        both(ev_q2, 1)
        both(ev_q2, 2)

        def pump(count):
            for _ in range(min(count, len(events))):
                events.pop(0)()

        def from_sibling():
            for kind in range(2):
                for dp in range(4):
                    for dq in range(4):
                        sibling(kind, dp, dq, True).wait_recv()

        def drain():
            for make, args in sent:
                make(*args).wait_send()

        return start, pump, from_sibling, drain

    full_start, full_pump, full_sibling, full_drain = make_ring(
        exp_v, red_v, False, send_sem, recv_sem, sib_send, sib_recv)
    half_start, half_pump, half_sibling, half_drain = make_ring(
        exp_h, red_h, True, hsend_sem, hrecv_sem, hsib_send, hsib_recv)

    halves = (seg == 0) | (seg == 3)
    active = ((seg == 0) & (core == 0)) | ((seg == 3) & (core == 1))

    def shard(kind):
        return pltpu.make_async_remote_copy(
            src_ref=own_src[kind], dst_ref=pane(exp_h, red_h, kind, lane // 2, None),
            send_sem=shard_send.at[kind], recv_sem=shard_recv.at[kind],
            device_id=((seg + 3) % 4, lane), device_id_type=MESH)

    def own_load(kind, exp_ref, red_ref, owner):
        return pltpu.make_async_copy(own_src[kind], pane(exp_ref, red_ref, kind, owner, None), local_sem.at[2 + kind])

    @pl.when((seg == 0) & (core == 1))
    def _():
        for kind in range(2):
            shard(kind).start()

    @pl.when((seg == 0) & (core == 0))
    def _():
        for kind in range(2):
            own_load(kind, exp_h, red_h, lane // 2).start()
        for kind in range(2):
            own_load(kind, exp_h, red_h, lane // 2).wait()

    @pl.when((seg == 3) & (core == 1))
    def _():
        for kind in range(2):
            shard(kind).wait_recv()

    @pl.when(active)
    def _():
        half_start()

    def norm_into(f, gain_ref):
        gain = gain_ref[...]
        for i in range(PAD // 16):
            rows = pl.ds(16 * i, 16)
            act[rows, :] = norm_rows(state[f, rows, :], gain).astype(BF)

    def project(f):
        norm_into(f, again_ref)

        for at in range(0, 3 * D, 256):
            packed[:, at:at + 256] = dot(act[...], trip_v[:, at:at + 256]).astype(BF)

    def attend():
        low = lax.broadcasted_iota(jnp.int32, (PAD, 128), 1) < 64
        bias = jnp.where(lax.broadcasted_iota(jnp.int32, (1, PAD), 1) < ROWS, 0.0, -1e30).astype(F32)

        for at in range(0, D, 128):
            q = packed[:, at:at + 128]
            k = packed[:, D + at:D + at + 128]
            v = packed[:, 2 * D + at:2 * D + at + 128]
            parts = []
            for keep in (low, ~low):
                scores = dot_t(jnp.where(keep, q * 0.125, 0.0).astype(BF), k) + bias
                shares = jnp.exp(scores - jnp.max(scores, axis=-1, keepdims=True))
                total = jnp.sum(shares, axis=-1, keepdims=True)
                parts.append(dot(shares.astype(BF), v) / total)
            ctx[:, at:at + 128] = jnp.where(low, parts[0], parts[1]).astype(BF)

    def join(f):
        for at in range(0, D, 256):
            state[f, :, at:at + 256] += dot(ctx[...], outw_v[:, at:at + 256])

    def feed(f, exp_ref, red_ref, depth):
        wide = dot(act[...], exp_ref[:, 0:256])
        for at in range(0, depth, 256):
            hidden = gelu(wide).astype(BF)
            if at + 256 < depth:
                wide = dot(act[...], exp_ref[:, at + 256:at + 512])
            state[f] += dot(hidden, red_ref[at:at + 256, :])

    for copy in loads[:2]:
        copy.wait()

    def relay(f):
        return pltpu.make_async_remote_copy(
            src_ref=outb.at[f], dst_ref=inb.at[f], send_sem=rel_send.at[f], recv_sem=rel_recv.at[f],
            device_id=((seg + 1) % 4, lane), device_id_type=MESH)

    def early(f):
        return pltpu.make_async_remote_copy(
            src_ref=outy.at[f], dst_ref=inb.at[f], send_sem=early_send.at[f], recv_sem=rel_recv.at[f],
            device_id=((seg + 3) % 4, lane), device_id_type=MESH)

    def partial(f):
        return pltpu.make_async_remote_copy(
            src_ref=outb.at[f], dst_ref=inp.at[f], send_sem=part_send.at[f], recv_sem=part_recv.at[f],
            device_id=((seg + 2) % 4, lane), device_id_type=MESH)

    @pl.when(halves)
    def _():
        for f in range(NF):
            @pl.when(seg == 0)
            def _():
                state[f, 192:PAD, :] = jnp.zeros((PAD - 192, D), F32)
                state[f, 0:ROWS, :] = frames_ref[f].astype(F32)
                project(f)

            @pl.when(active)
            def _():
                half_pump(4)

            @pl.when(seg == 0)
            def _():
                attend()

            @pl.when(active)
            def _():
                half_pump(4)

            @pl.when(seg == 0)
            def _():
                join(f)
                norm_into(f, dgain_ref)
                outy[f] = act[...]
                early(f).start()

            @pl.when(active)
            def _():
                half_pump(2)

        @pl.when(active)
        def _():
            half_pump(1000)

        @pl.when(~active)
        def _():
            half_sibling()

        def step(f, carry):
            @pl.when(seg == 3)
            def _():
                early(f).wait_recv()
                act[...] = inb[f]
                state[f] = jnp.zeros((PAD, D), F32)

            @pl.when(seg == 0)
            def _():
                act[...] = outy[f]

            feed(f, exp_h, red_h, FF // 2)
            outb[f] = state[f].astype(BF)

            @pl.when(seg == 0)
            def _():
                relay(f).start()

            @pl.when(seg == 3)
            def _():
                partial(f).start()

            return carry

        lax.fori_loop(0, NF, step, 0)

    @pl.when(seg > 0)
    def _():
        full_start()
        for kind in range(2):
            own_load(kind, exp_v, red_v, lane).start()
        full_pump(1000)
        full_sibling()
        for kind in range(2):
            own_load(kind, exp_v, red_v, lane).wait()

    @pl.when(seg == 2)
    def _():
        pooled[...] = jnp.zeros_like(pooled)

    @pl.when((seg == 1) | (seg == 2))
    def _():
        def step(f, carry):
            relay(f).wait_recv()

            @pl.when(seg == 2)
            def _():
                state[f] = inb[f].astype(F32)

            @pl.when(seg == 1)
            def _():
                partial(f).wait_recv()
                state[f] = inb[f].astype(F32) + inp[f].astype(F32)

            project(f)
            attend()
            join(f)
            norm_into(f, dgain_ref)
            feed(f, exp_v, red_v, FF)

            @pl.when(seg == 1)
            def _():
                outb[f] = state[f].astype(BF)
                relay(f).start()

            @pl.when(seg == 2)
            def _():
                gain = fgain_ref[...]
                total = jnp.zeros((16, D), F32)
                for i in range(PAD // 16):
                    rows = norm_rows(state[f, pl.ds(16 * i, 16), :], gain)
                    if 16 * i + 16 > ROWS:
                        keep = lax.broadcasted_iota(jnp.int32, (16, D), 0) < ROWS - 16 * i
                        rows = jnp.where(keep, rows, 0.0)
                    total = total + rows
                pooled[pl.ds(f, 1), :] = jnp.sum(total, axis=0, keepdims=True) * (1.0 / ROWS)

            return carry

        lax.fori_loop(0, NF, step, 0)

    def pool_copy(d):
        return pltpu.make_async_remote_copy(
            src_ref=pooled, dst_ref=pin.at[pl.ds(8 * (d + REACH), 8), :],
            send_sem=pool_send.at[d + REACH], recv_sem=pool_recv.at[d + REACH],
            device_id=((seg + 1) % 4, (lane - d + 32) % 32), device_id_type=MESH)

    def result_copy(section):
        return pltpu.make_async_remote_copy(
            src_ref=obuf.at[section], dst_ref=rbuf, send_sem=fin_send.at[section], recv_sem=fin_recv,
            device_id=(section, lane), device_id_type=MESH)

    @pl.when(seg == 2)
    def _():
        for d in range(-REACH, REACH + 1):
            pool_copy(d).start()

    @pl.when(seg == 3)
    def _():
        pin[8 * SLOTS:KEYS, :] = jnp.zeros((KEYS - 8 * SLOTS, D), F32)
        for d in range(-REACH, REACH + 1):
            pool_copy(d).wait_recv()
        again = again_ref[...]
        for i in range(KEYS // 16):
            rows = pl.ds(16 * i, 16)
            act[rows, :] = norm_rows(pin[rows, :], again).astype(BF)

        for at in range(0, 3 * D, 256):
            packed[0:KEYS, at:at + 256] = dot(act[0:KEYS, :], trip_v[:, at:at + 256]).astype(BF)

        col = lax.broadcasted_iota(jnp.int32, (16, KEYS), 1)
        row = lax.broadcasted_iota(jnp.int32, (16, KEYS), 0)
        key_lane = (lane + (col >> 3) - REACH + 32) & 31
        key_at = key_lane * NF + (col & 7)
        own_at = lane * NF + jnp.minimum(row, NF - 1)
        key_shot = jnp.zeros((16, KEYS), jnp.int32)
        own_shot = jnp.zeros((16, KEYS), jnp.int32)
        end = 0
        for s in range(24):
            end = end + shot_ref[s]
            key_shot += (key_at >= end).astype(jnp.int32)
            own_shot += (own_at >= end).astype(jnp.int32)
        allowed = (key_shot == own_shot) & ((col & 7) < NF) & (col < 8 * SLOTS)
        low = lax.broadcasted_iota(jnp.int32, (16, 128), 1) < 64
        mine = 8 * REACH

        for at in range(0, D, 128):
            q = packed[mine:mine + 16, at:at + 128]
            k = packed[0:KEYS, D + at:D + at + 128]
            v = packed[0:KEYS, 2 * D + at:2 * D + at + 128]
            parts = []
            for keep in (low, ~low):
                scores = dot_t(jnp.where(keep, q * 0.125, 0.0).astype(BF), k)
                scores = jnp.where(allowed, scores, -1e30)
                shares = jnp.exp(scores - jnp.max(scores, axis=-1, keepdims=True))
                total = jnp.sum(shares, axis=-1, keepdims=True)
                high = shares.astype(BF)
                rest = (shares - high.astype(F32)).astype(BF)
                parts.append((dot(high, v) + dot(rest, v)) / total)
            ctx[0:16, at:at + 128] = jnp.where(low, parts[0], parts[1]).astype(BF)

        temporal = pin[mine:mine + 16, :] + dot(ctx[0:16, :], outw_v[...])
        act[0:16, :] = norm_rows(temporal, dgain_ref[...]).astype(BF)

        wide = dot(act[0:16, :], exp_v[:, 0:256])
        for at in range(0, FF, 256):
            hidden = gelu(wide).astype(BF)
            if at + 256 < FF:
                wide = dot(act[0:16, :], exp_v[:, at + 256:at + 512])
            temporal = temporal + dot(hidden, red_v[at:at + 256, :])

        for section in range(4):
            obuf[section] = temporal[0:8, 256 * section:256 * section + 256]
        for section in range(3):
            result_copy(section).start()
        out_ref[...] = obuf[3, 0:NF, :]
        for section in range(3):
            result_copy(section).wait_send()

    @pl.when(seg == 2)
    def _():
        for d in range(-REACH, REACH + 1):
            pool_copy(d).wait_send()

    @pl.when(seg < 2)
    def _():
        for f in range(NF):
            relay(f).wait_send()

    @pl.when(seg == 0)
    def _():
        for f in range(NF):
            early(f).wait_send()

    @pl.when(seg == 3)
    def _():
        for f in range(NF):
            partial(f).wait_send()

    @pl.when((seg == 0) & (core == 1))
    def _():
        for kind in range(2):
            shard(kind).wait_send()

    @pl.when(active)
    def _():
        half_drain()

    @pl.when(seg > 0)
    def _():
        full_drain()

    @pl.when(seg < 3)
    def _():
        result_copy(0).wait_recv()
        out_ref[...] = rbuf[0:NF, :]


def body(frames, triple_weight, output_weight, expand_weight, reduce_weight, attend_gain, dense_gain, final_gain, shot_lengths):
    vmem = pl.BlockSpec(memory_space=pltpu.VMEM)
    anywhere = pl.BlockSpec(memory_space=pl.ANY)
    dma = pltpu.SemaphoreType.DMA
    return pl.pallas_call(
        kernel,
        out_shape=jax.ShapeDtypeStruct((NF, 256), F32),
        in_specs=[vmem, anywhere, anywhere, anywhere, anywhere, vmem, vmem, vmem,
                  pl.BlockSpec(memory_space=pltpu.SMEM)],
        out_specs=vmem,
        scratch_shapes=[
            pltpu.VMEM((D, FF), BF), pltpu.VMEM((FF, D), BF),
            pltpu.VMEM((D, FF // 2), BF), pltpu.VMEM((FF // 2, D), BF), pltpu.VMEM((D, 3 * D), BF), pltpu.VMEM((D, D), BF),
            pltpu.VMEM((NF, PAD, D), F32), pltpu.VMEM((NF, PAD, D), BF), pltpu.VMEM((NF, PAD, D), BF),
            pltpu.VMEM((NF, PAD, D), BF), pltpu.VMEM((NF, PAD, D), BF),
            pltpu.VMEM((PAD, 3 * D), BF), pltpu.VMEM((PAD, D), BF), pltpu.VMEM((PAD, D), BF),
            pltpu.VMEM((8, D), F32), pltpu.VMEM((KEYS, D), F32), pltpu.VMEM((4, 8, 256), F32), pltpu.VMEM((8, 256), F32),
            dma((4,)), dma((2, 4, 4, 2)), dma((2, 4, 4, 2)), dma((2, 4, 4)), dma((2, 4, 4)),
            dma((2, 4, 4, 2)), dma((2, 4, 4, 2)), dma((2, 4, 4)), dma((2, 4, 4)),
            dma((NF,)), dma((NF,)), dma((NF,)), dma((NF,)), dma((NF,)), dma((2,)), dma((2,)),
            dma((SLOTS,)), dma((SLOTS,)), dma((3,)), dma(()),
        ],
        compiler_params=pltpu.CompilerParams(
            collective_id=0, has_side_effects=True, vmem_limit_bytes=60 * 1024 * 1024),
    )(frames, triple_weight, output_weight, expand_weight, reduce_weight, attend_gain, dense_gain,
      final_gain.reshape(1, D), shot_lengths)


def solution(mesh):
    return jax.shard_map(
        body,
        mesh=mesh,
        in_specs=(
            P("lane", None, None),
            P("segment", None, None),
            P("segment", None, None),
            P("segment", None, "lane"),
            P("segment", "lane", None),
            P("segment", None),
            P("segment", None),
            P(),
            P(),
        ),
        out_specs=P("lane", "segment"),
        check_vma=False,
    )
```

time: 142 us -> 121 us (0.85)
  Pallas kernels: 140 us -> 120 us
    pallas_call x1, Pallas kernels: 140 us -> 120 us  [body(): pl.pallas_call(kernel, out_shape=jax.ShapeDtypeStruct((NF, 256), F32), in...]
where the time goes in v3:
time: 121 us
  Pallas kernels  120 us (99%)
  local copies, waits for them, and re-layouts  1.28 us (1%)
    pallas_call x1, Pallas kernels, body(): pl.pallas_call(kernel, out_shape=jax.ShapeDtypeStruct((NF, 256), F32), in...  120 us

profile of v3, /device:TPU:0, one launch (start us, length us, event | category | flops | bytes accessed | tf_op | source)
XLA Modules:
  0.0 121.0 jit_solution(1012278280271921844)
XLA Ops:
  0.0 119.7 %shard_map.91 = f32[3,256]{1,0:T(4,128)} custom-call(bf16[3,197,1024]{2,1,0:T(8,128)(2,1)} %frames_ref.1, bf16[1,1024,3072]{2,1,0:T(8,128)(2,1)} %triple_hbm.1, bf16[1,1024,1024]{2,1,0:T(8,128)(2,1)} %output_hbm.1, bf16[1,1024,128]{2,1,0:T(8,128)(2,1)} %expand_hbm.1, bf16[1,128,1024]{2,1,0:T(8,128)(2,1)} %reduce_hbm.1, f32[1,1024]{1,0:T(1,128)} %again_ref.1, ...), custom_call_target="tpu_custom_call" | custom-call | tf_op jit(solution)/shard_map/pallas_call | solution.py:545
  119.7 1.3 %copy.11 = f32[3,256]{1,0:T(4,128)} copy(f32[3,256]{1,0:T(4,128)} %shard_map.91) | data formatting | bytes 6144

commit v4 on v3

--- a/solution.py
+++ b/solution.py
@@ -11,12 +11,14 @@
 HEADS = 16
 ROWS = 197
 PAD = 208
+SENT = 200
 D = 1024
 FF = 4096
 NF = 3
 REACH = 4
 SLOTS = 2 * REACH + 1
-KEYS = 80
+KEYS = 32
+MINE = NF * REACH
 MESH = pl.DeviceIdType.MESH
 F32 = jnp.float32
 BF = jnp.bfloat16
@@ -65,6 +67,10 @@
     for copy in loads:
         copy.start()
 
+    for f in range(NF):
+        inb[f, 192:PAD, :] = jnp.zeros((PAD - 192, D), BF)
+        inp[f, 192:PAD, :] = jnp.zeros((PAD - 192, D), BF)
+
     peers = [
         (seg, lane_at(cx + 1, cz, core)), (seg, lane_at(cx + 3, cz, core)),
         (seg, lane_at(cx, cz + 1, core)), (seg, lane_at(cx, cz + 3, core)),
@@ -132,8 +138,10 @@
             make(*args).start()
             sent.append((make, args))
 
-        def start():
+        def start(ready=None):
             for kind in range(2):
+                if ready is not None:
+                    ready(kind)
                 for sign in (1, -1):
                     go(hop, kind, 0, 0, None, True, sign)
             for kind in range(2):
@@ -230,17 +238,19 @@
     def _():
         for kind in range(2):
             own_load(kind, exp_h, red_h, lane // 2).start()
-        for kind in range(2):
+
+    def ready(kind):
+        @pl.when(seg == 0)
+        def _():
             own_load(kind, exp_h, red_h, lane // 2).wait()
 
-    @pl.when((seg == 3) & (core == 1))
-    def _():
-        for kind in range(2):
+        @pl.when(seg == 3)
+        def _():
             shard(kind).wait_recv()
 
     @pl.when(active)
     def _():
-        half_start()
+        half_start(ready)
 
     def norm_into(f, gain_ref):
         gain = gain_ref[...]
@@ -287,17 +297,17 @@
 
     def relay(f):
         return pltpu.make_async_remote_copy(
-            src_ref=outb.at[f], dst_ref=inb.at[f], send_sem=rel_send.at[f], recv_sem=rel_recv.at[f],
+            src_ref=outb.at[f, 0:SENT, :], dst_ref=inb.at[f, 0:SENT, :], send_sem=rel_send.at[f], recv_sem=rel_recv.at[f],
             device_id=((seg + 1) % 4, lane), device_id_type=MESH)
 
     def early(f):
         return pltpu.make_async_remote_copy(
-            src_ref=outy.at[f], dst_ref=inb.at[f], send_sem=early_send.at[f], recv_sem=rel_recv.at[f],
+            src_ref=outy.at[f, 0:SENT, :], dst_ref=inb.at[f, 0:SENT, :], send_sem=early_send.at[f], recv_sem=rel_recv.at[f],
             device_id=((seg + 3) % 4, lane), device_id_type=MESH)
 
     def partial(f):
         return pltpu.make_async_remote_copy(
-            src_ref=outb.at[f], dst_ref=inp.at[f], send_sem=part_send.at[f], recv_sem=part_recv.at[f],
+            src_ref=outb.at[f, 0:SENT, :], dst_ref=inp.at[f, 0:SENT, :], send_sem=part_send.at[f], recv_sem=part_recv.at[f],
             device_id=((seg + 2) % 4, lane), device_id_type=MESH)
 
     @pl.when(halves)
@@ -372,13 +382,17 @@
         for kind in range(2):
             own_load(kind, exp_v, red_v, lane).start()
         full_pump(1000)
+
+    def gathered():
         full_sibling()
         for kind in range(2):
             own_load(kind, exp_v, red_v, lane).wait()
 
-    @pl.when(seg == 2)
-    def _():
-        pooled[...] = jnp.zeros_like(pooled)
+    def pool_copy(f, d):
+        return pltpu.make_async_remote_copy(
+            src_ref=pooled.at[f], dst_ref=pin.at[d + REACH, f],
+            send_sem=pool_send.at[f, d + REACH], recv_sem=pool_recv.at[f, d + REACH],
+            device_id=((seg + 1) % 4, (lane - d + 32) % 32), device_id_type=MESH)
 
     @pl.when((seg == 1) | (seg == 2))
     def _():
@@ -398,6 +412,11 @@
             attend()
             join(f)
             norm_into(f, dgain_ref)
+
+            @pl.when(f == 0)
+            def _():
+                gathered()
+
             feed(f, exp_v, red_v, FF)
 
             @pl.when(seg == 1)
@@ -415,46 +434,45 @@
                         keep = lax.broadcasted_iota(jnp.int32, (16, D), 0) < ROWS - 16 * i
                         rows = jnp.where(keep, rows, 0.0)
                     total = total + rows
-                pooled[pl.ds(f, 1), :] = jnp.sum(total, axis=0, keepdims=True) * (1.0 / ROWS)
+                total = jnp.sum(total, axis=0, keepdims=True) * (1.0 / ROWS)
+                for j in range(8):
+                    pooled[f, j:j + 1, :] = total[:, 128 * j:128 * j + 128]
+                for d in range(-REACH, REACH + 1):
+                    pool_copy(f, d).start()
 
             return carry
 
         lax.fori_loop(0, NF, step, 0)
-
-    def pool_copy(d):
-        return pltpu.make_async_remote_copy(
-            src_ref=pooled, dst_ref=pin.at[pl.ds(8 * (d + REACH), 8), :],
-            send_sem=pool_send.at[d + REACH], recv_sem=pool_recv.at[d + REACH],
-            device_id=((seg + 1) % 4, (lane - d + 32) % 32), device_id_type=MESH)
 
     def result_copy(section):
         return pltpu.make_async_remote_copy(
             src_ref=obuf.at[section], dst_ref=rbuf, send_sem=fin_send.at[section], recv_sem=fin_recv,
             device_id=(section, lane), device_id_type=MESH)
 
-    @pl.when(seg == 2)
-    def _():
-        for d in range(-REACH, REACH + 1):
-            pool_copy(d).start()
-
     @pl.when(seg == 3)
     def _():
-        pin[8 * SLOTS:KEYS, :] = jnp.zeros((KEYS - 8 * SLOTS, D), F32)
-        for d in range(-REACH, REACH + 1):
-            pool_copy(d).wait_recv()
+        gathered()
+        state[0, 24:KEYS, :] = jnp.zeros((KEYS - 24, D), F32)
+        for f in range(NF):
+            for d in range(-REACH, REACH + 1):
+                pool_copy(f, d).wait_recv()
+                row = NF * (d + REACH) + f
+                for j in range(8):
+                    state[0, row:row + 1, 128 * j:128 * j + 128] = pin[d + REACH, f, j:j + 1, :]
         again = again_ref[...]
         for i in range(KEYS // 16):
             rows = pl.ds(16 * i, 16)
-            act[rows, :] = norm_rows(pin[rows, :], again).astype(BF)
+            act[rows, :] = norm_rows(state[0, rows, :], again).astype(BF)
 
         for at in range(0, 3 * D, 256):
             packed[0:KEYS, at:at + 256] = dot(act[0:KEYS, :], trip_v[:, at:at + 256]).astype(BF)
 
         col = lax.broadcasted_iota(jnp.int32, (16, KEYS), 1)
         row = lax.broadcasted_iota(jnp.int32, (16, KEYS), 0)
-        key_lane = (lane + (col >> 3) - REACH + 32) & 31
-        key_at = key_lane * NF + (col & 7)
-        own_at = lane * NF + jnp.minimum(row, NF - 1)
+        key_at = (lane - REACH) * NF + col
+        key_at = jnp.where(key_at < 0, key_at + 32 * NF, key_at)
+        key_at = jnp.where(key_at >= 32 * NF, key_at - 32 * NF, key_at)
+        own_at = lane * NF + jnp.clip(row - MINE, 0, NF - 1)
         key_shot = jnp.zeros((16, KEYS), jnp.int32)
         own_shot = jnp.zeros((16, KEYS), jnp.int32)
         end = 0
@@ -462,12 +480,11 @@
             end = end + shot_ref[s]
             key_shot += (key_at >= end).astype(jnp.int32)
             own_shot += (own_at >= end).astype(jnp.int32)
-        allowed = (key_shot == own_shot) & ((col & 7) < NF) & (col < 8 * SLOTS)
+        allowed = (key_shot == own_shot) & (col < NF * SLOTS)
         low = lax.broadcasted_iota(jnp.int32, (16, 128), 1) < 64
-        mine = 8 * REACH
 
         for at in range(0, D, 128):
-            q = packed[mine:mine + 16, at:at + 128]
+            q = packed[0:16, at:at + 128]
             k = packed[0:KEYS, D + at:D + at + 128]
             v = packed[0:KEYS, 2 * D + at:2 * D + at + 128]
             parts = []
@@ -481,7 +498,7 @@
                 parts.append((dot(high, v) + dot(rest, v)) / total)
             ctx[0:16, at:at + 128] = jnp.where(low, parts[0], parts[1]).astype(BF)
 
-        temporal = pin[mine:mine + 16, :] + dot(ctx[0:16, :], outw_v[...])
+        temporal = state[0, 0:16, :] + dot(ctx[0:16, :], outw_v[...])
         act[0:16, :] = norm_rows(temporal, dgain_ref[...]).astype(BF)
 
         wide = dot(act[0:16, :], exp_v[:, 0:256])
@@ -492,17 +509,18 @@
             temporal = temporal + dot(hidden, red_v[at:at + 256, :])
 
         for section in range(4):
-            obuf[section] = temporal[0:8, 256 * section:256 * section + 256]
+            obuf[section] = temporal[8:16, 256 * section:256 * section + 256]
         for section in range(3):
             result_copy(section).start()
-        out_ref[...] = obuf[3, 0:NF, :]
+        out_ref[...] = obuf[3, MINE - 8:MINE - 8 + NF, :]
         for section in range(3):
             result_copy(section).wait_send()
 
     @pl.when(seg == 2)
     def _():
-        for d in range(-REACH, REACH + 1):
-            pool_copy(d).wait_send()
+        for f in range(NF):
+            for d in range(-REACH, REACH + 1):
+                pool_copy(f, d).wait_send()
 
     @pl.when(seg < 2)
     def _():
@@ -535,7 +553,7 @@
     @pl.when(seg < 3)
     def _():
         result_copy(0).wait_recv()
-        out_ref[...] = rbuf[0:NF, :]
+        out_ref[...] = rbuf[MINE - 8:MINE - 8 + NF, :]
 
 
 def body(frames, triple_weight, output_weight, expand_weight, reduce_weight, attend_gain, dense_gain, final_gain, shot_lengths):
@@ -554,11 +572,11 @@
             pltpu.VMEM((NF, PAD, D), F32), pltpu.VMEM((NF, PAD, D), BF), pltpu.VMEM((NF, PAD, D), BF),
             pltpu.VMEM((NF, PAD, D), BF), pltpu.VMEM((NF, PAD, D), BF),
             pltpu.VMEM((PAD, 3 * D), BF), pltpu.VMEM((PAD, D), BF), pltpu.VMEM((PAD, D), BF),
-            pltpu.VMEM((8, D), F32), pltpu.VMEM((KEYS, D), F32), pltpu.VMEM((4, 8, 256), F32), pltpu.VMEM((8, 256), F32),
+            pltpu.VMEM((NF, 8, 128), F32), pltpu.VMEM((SLOTS, NF, 8, 128), F32), pltpu.VMEM((4, 8, 256), F32), pltpu.VMEM((8, 256), F32),
             dma((4,)), dma((2, 4, 4, 2)), dma((2, 4, 4, 2)), dma((2, 4, 4)), dma((2, 4, 4)),
             dma((2, 4, 4, 2)), dma((2, 4, 4, 2)), dma((2, 4, 4)), dma((2, 4, 4)),
             dma((NF,)), dma((NF,)), dma((NF,)), dma((NF,)), dma((NF,)), dma((2,)), dma((2,)),
-            dma((SLOTS,)), dma((SLOTS,)), dma((3,)), dma(()),
+            dma((NF, SLOTS)), dma((NF, SLOTS)), dma((3,)), dma(()),
         ],
         compiler_params=pltpu.CompilerParams(
             collective_id=0, has_side_effects=True, vmem_limit_bytes=60 * 1024 * 1024),

time: 121 us -> 115 us (0.950)
  Pallas kernels: 120 us -> 114 us
    pallas_call x1, Pallas kernels: 120 us -> 114 us  [body(): pl.pallas_call(kernel, out_shape=jax.ShapeDtypeStruct((NF, 256), F32), in...]
where the time goes in v4:
time: 115 us
  Pallas kernels  114 us (99%)
  local copies, waits for them, and re-layouts  1.28 us (1%)
    pallas_call x1, Pallas kernels, body(): pl.pallas_call(kernel, out_shape=jax.ShapeDtypeStruct((NF, 256), F32), in...  114 us

profile of v4, /device:TPU:0, one launch (start us, length us, event | category | flops | bytes accessed | tf_op | source)
XLA Modules:
  0.0 115.1 jit_solution(2993172331089153233)
XLA Ops:
  0.0 113.9 %shard_map.91 = f32[3,256]{1,0:T(4,128)} custom-call(bf16[3,197,1024]{2,1,0:T(8,128)(2,1)} %frames_ref.1, bf16[1,1024,3072]{2,1,0:T(8,128)(2,1)} %triple_hbm.1, bf16[1,1024,1024]{2,1,0:T(8,128)(2,1)} %output_hbm.1, bf16[1,1024,128]{2,1,0:T(8,128)(2,1)} %expand_hbm.1, bf16[1,128,1024]{2,1,0:T(8,128)(2,1)} %reduce_hbm.1, f32[1,1024]{1,0:T(1,128)} %again_ref.1, ...), custom_call_target="tpu_custom_call" | custom-call | tf_op jit(solution)/shard_map/pallas_call | solution.py:563
  113.9 1.3 %copy.11 = f32[3,256]{1,0:T(4,128)} copy(f32[3,256]{1,0:T(4,128)} %shard_map.91) | data formatting | bytes 6144

commit v5 on v4

--- a/solution.py
+++ b/solution.py
@@ -44,11 +44,11 @@
 
 
 def kernel(
-    frames_ref, triple_hbm, output_hbm, expand_hbm, reduce_hbm, again_ref, dgain_ref, fgain_ref, shot_ref,
+    frames_hbm, triple_hbm, output_hbm, expand_hbm, reduce_hbm, again_ref, dgain_ref, fgain_ref, shot_ref,
     out_ref,
-    exp_v, red_v, exp_h, red_h, trip_v, outw_v, state, inb, inp, outb, outy, packed, act, ctx, pooled, pin, obuf, rbuf,
+    exp_v, red_v, exp_h, red_h, trip_v, outw_v, frames_v, hid, state, inb, outb, outy, packed, act, ctx, pooled, pin, obuf, rbuf,
     local_sem, send_sem, recv_sem, sib_send, sib_recv, hsend_sem, hrecv_sem, hsib_send, hsib_recv,
-    rel_send, rel_recv, early_send, part_send, part_recv, shard_send, shard_recv,
+    rel_send, rel_recv, early_send, early_recv, shard_send, shard_recv,
     pool_send, pool_recv, fin_send, fin_recv,
 ):
     seg = lax.axis_index("segment")
@@ -63,13 +63,14 @@
     loads = [
         pltpu.make_async_copy(triple_hbm.at[0], trip_v, local_sem.at[0]),
         pltpu.make_async_copy(output_hbm.at[0], outw_v, local_sem.at[1]),
+        pltpu.make_async_copy(frames_hbm, frames_v, local_sem.at[4]),
     ]
     for copy in loads:
         copy.start()
 
     for f in range(NF):
-        inb[f, 192:PAD, :] = jnp.zeros((PAD - 192, D), BF)
-        inp[f, 192:PAD, :] = jnp.zeros((PAD - 192, D), BF)
+        for way in range(2):
+            inb[way, f, 192:PAD, :] = jnp.zeros((PAD - 192, D), BF)
 
     peers = [
         (seg, lane_at(cx + 1, cz, core)), (seg, lane_at(cx + 3, cz, core)),
@@ -136,7 +137,8 @@
 
         def go(make, *args):
             make(*args).start()
-            sent.append((make, args))
+            if (make, args) not in sent:
+                sent.append((make, args))
 
         def start(ready=None):
             for kind in range(2):
@@ -284,31 +286,38 @@
         for at in range(0, D, 256):
             state[f, :, at:at + 256] += dot(ctx[...], outw_v[:, at:at + 256])
 
-    def feed(f, exp_ref, red_ref, depth):
+    def feed(f, exp_ref, red_ref, depth, emit):
         wide = dot(act[...], exp_ref[:, 0:256])
         for at in range(0, depth, 256):
             hidden = gelu(wide).astype(BF)
             if at + 256 < depth:
                 wide = dot(act[...], exp_ref[:, at + 256:at + 512])
-            state[f] += dot(hidden, red_ref[at:at + 256, :])
-
-    for copy in loads[:2]:
+            hid[:, at:at + 256] = hidden
+        for c in range(4):
+            cols = slice(256 * c, 256 * c + 256)
+            emit(c, cols, state[f, :, cols] + dot(hid[:, 0:depth], red_ref[:, cols]))
+
+    for copy in loads:
         copy.wait()
 
-    def relay(f):
+    def relay(f, c, way, section):
+        cols = slice(256 * c, 256 * c + 256)
         return pltpu.make_async_remote_copy(
-            src_ref=outb.at[f, 0:SENT, :], dst_ref=inb.at[f, 0:SENT, :], send_sem=rel_send.at[f], recv_sem=rel_recv.at[f],
-            device_id=((seg + 1) % 4, lane), device_id_type=MESH)
+            src_ref=outb.at[f, 0:SENT, cols], dst_ref=inb.at[way, f, 0:SENT, cols],
+            send_sem=rel_send.at[f, c], recv_sem=rel_recv.at[way, f, c],
+            device_id=(section, lane), device_id_type=MESH)
+
+    def pass_on(f, way, section):
+        def emit(c, cols, value):
+            outb[f, :, cols] = value.astype(BF)
+            relay(f, c, way, section).start()
+
+        return emit
 
     def early(f):
         return pltpu.make_async_remote_copy(
-            src_ref=outy.at[f, 0:SENT, :], dst_ref=inb.at[f, 0:SENT, :], send_sem=early_send.at[f], recv_sem=rel_recv.at[f],
+            src_ref=outy.at[f, 0:SENT, :], dst_ref=inb.at[0, f, 0:SENT, :], send_sem=early_send.at[f], recv_sem=early_recv.at[f],
             device_id=((seg + 3) % 4, lane), device_id_type=MESH)
-
-    def partial(f):
-        return pltpu.make_async_remote_copy(
-            src_ref=outb.at[f, 0:SENT, :], dst_ref=inp.at[f, 0:SENT, :], send_sem=part_send.at[f], recv_sem=part_recv.at[f],
-            device_id=((seg + 2) % 4, lane), device_id_type=MESH)
 
     @pl.when(halves)
     def _():
@@ -316,7 +325,7 @@
             @pl.when(seg == 0)
             def _():
                 state[f, 192:PAD, :] = jnp.zeros((PAD - 192, D), F32)
-                state[f, 0:ROWS, :] = frames_ref[f].astype(F32)
+                state[f, 0:ROWS, :] = frames_v[f].astype(F32)
                 project(f)
 
             @pl.when(active)
@@ -350,35 +359,32 @@
         def _():
             half_sibling()
 
+        @pl.when(seg == 3)
+        def _():
+            full_start()
+
         def step(f, carry):
             @pl.when(seg == 3)
             def _():
                 early(f).wait_recv()
-                act[...] = inb[f]
+                act[...] = inb[0, f]
                 state[f] = jnp.zeros((PAD, D), F32)
 
             @pl.when(seg == 0)
             def _():
                 act[...] = outy[f]
 
-            feed(f, exp_h, red_h, FF // 2)
-            outb[f] = state[f].astype(BF)
-
-            @pl.when(seg == 0)
-            def _():
-                relay(f).start()
-
-            @pl.when(seg == 3)
-            def _():
-                partial(f).start()
-
+            feed(f, exp_h, red_h, FF // 2, pass_on(f, seg // 3, 1))
             return carry
 
         lax.fori_loop(0, NF, step, 0)
 
+    @pl.when((seg == 1) | (seg == 2))
+    def _():
+        full_start()
+
     @pl.when(seg > 0)
     def _():
-        full_start()
         for kind in range(2):
             own_load(kind, exp_v, red_v, lane).start()
         full_pump(1000)
@@ -397,16 +403,18 @@
     @pl.when((seg == 1) | (seg == 2))
     def _():
         def step(f, carry):
-            relay(f).wait_recv()
+            for c in range(4):
+                relay(f, c, 0, 2).wait_recv()
 
             @pl.when(seg == 2)
             def _():
-                state[f] = inb[f].astype(F32)
+                state[f] = inb[0, f].astype(F32)
 
             @pl.when(seg == 1)
             def _():
-                partial(f).wait_recv()
-                state[f] = inb[f].astype(F32) + inp[f].astype(F32)
+                for c in range(4):
+                    relay(f, c, 1, 2).wait_recv()
+                state[f] = inb[0, f].astype(F32) + inb[1, f].astype(F32)
 
             project(f)
             attend()
@@ -417,15 +425,16 @@
             def _():
                 gathered()
 
-            feed(f, exp_v, red_v, FF)
-
             @pl.when(seg == 1)
             def _():
-                outb[f] = state[f].astype(BF)
-                relay(f).start()
+                feed(f, exp_v, red_v, FF, pass_on(f, 0, 2))
 
             @pl.when(seg == 2)
             def _():
+                def keep_block(c, cols, value):
+                    state[f, :, cols] = value
+
+                feed(f, exp_v, red_v, FF, keep_block)
                 gain = fgain_ref[...]
                 total = jnp.zeros((16, D), F32)
                 for i in range(PAD // 16):
@@ -451,7 +460,6 @@
 
     @pl.when(seg == 3)
     def _():
-        gathered()
         state[0, 24:KEYS, :] = jnp.zeros((KEYS - 24, D), F32)
         for f in range(NF):
             for d in range(-REACH, REACH + 1):
@@ -501,6 +509,7 @@
         temporal = state[0, 0:16, :] + dot(ctx[0:16, :], outw_v[...])
         act[0:16, :] = norm_rows(temporal, dgain_ref[...]).astype(BF)
 
+        gathered()
         wide = dot(act[0:16, :], exp_v[:, 0:256])
         for at in range(0, FF, 256):
             hidden = gelu(wide).astype(BF)
@@ -525,7 +534,8 @@
     @pl.when(seg < 2)
     def _():
         for f in range(NF):
-            relay(f).wait_send()
+            for c in range(4):
+                relay(f, c, 0, 1).wait_send()
 
     @pl.when(seg == 0)
     def _():
@@ -535,7 +545,8 @@
     @pl.when(seg == 3)
     def _():
         for f in range(NF):
-            partial(f).wait_send()
+            for c in range(4):
+                relay(f, c, 1, 1).wait_send()
 
     @pl.when((seg == 0) & (core == 1))
     def _():
@@ -563,19 +574,20 @@
     return pl.pallas_call(
         kernel,
         out_shape=jax.ShapeDtypeStruct((NF, 256), F32),
-        in_specs=[vmem, anywhere, anywhere, anywhere, anywhere, vmem, vmem, vmem,
+        in_specs=[anywhere, anywhere, anywhere, anywhere, anywhere, vmem, vmem, vmem,
                   pl.BlockSpec(memory_space=pltpu.SMEM)],
         out_specs=vmem,
         scratch_shapes=[
             pltpu.VMEM((D, FF), BF), pltpu.VMEM((FF, D), BF),
             pltpu.VMEM((D, FF // 2), BF), pltpu.VMEM((FF // 2, D), BF), pltpu.VMEM((D, 3 * D), BF), pltpu.VMEM((D, D), BF),
-            pltpu.VMEM((NF, PAD, D), F32), pltpu.VMEM((NF, PAD, D), BF), pltpu.VMEM((NF, PAD, D), BF),
+            pltpu.VMEM((NF, ROWS, D), BF), pltpu.VMEM((PAD, FF), BF),
+            pltpu.VMEM((NF, PAD, D), F32), pltpu.VMEM((2, NF, PAD, D), BF),
             pltpu.VMEM((NF, PAD, D), BF), pltpu.VMEM((NF, PAD, D), BF),
             pltpu.VMEM((PAD, 3 * D), BF), pltpu.VMEM((PAD, D), BF), pltpu.VMEM((PAD, D), BF),
             pltpu.VMEM((NF, 8, 128), F32), pltpu.VMEM((SLOTS, NF, 8, 128), F32), pltpu.VMEM((4, 8, 256), F32), pltpu.VMEM((8, 256), F32),
-            dma((4,)), dma((2, 4, 4, 2)), dma((2, 4, 4, 2)), dma((2, 4, 4)), dma((2, 4, 4)),
+            dma((5,)), dma((2, 4, 4, 2)), dma((2, 4, 4, 2)), dma((2, 4, 4)), dma((2, 4, 4)),
             dma((2, 4, 4, 2)), dma((2, 4, 4, 2)), dma((2, 4, 4)), dma((2, 4, 4)),
-            dma((NF,)), dma((NF,)), dma((NF,)), dma((NF,)), dma((NF,)), dma((2,)), dma((2,)),
+            dma((NF, 4)), dma((2, NF, 4)), dma((NF,)), dma((NF,)), dma((2,)), dma((2,)),
             dma((NF, SLOTS)), dma((NF, SLOTS)), dma((3,)), dma(()),
         ],
         compiler_params=pltpu.CompilerParams(

time: 115 us -> 116 us (level)
  no operation moved by 1% of the time
where the time goes in v5:
time: 116 us
  Pallas kernels  115 us (99%)
  local copies, waits for them, and re-layouts  1.28 us (1%)
    pallas_call x1, Pallas kernels, body(): pl.pallas_call(kernel, out_shape=jax.ShapeDtypeStruct((NF, 256), F32), in...  115 us

profile of v5, /device:TPU:0, one launch (start us, length us, event | category | flops | bytes accessed | tf_op | source)
XLA Modules:
  0.0 116.0 jit_solution(17067791514917819877)
XLA Ops:
  0.0 114.7 %shard_map.91 = f32[3,256]{1,0:T(4,128)} custom-call(bf16[3,197,1024]{2,1,0:T(8,128)(2,1)} %frames_hbm.1, bf16[1,1024,3072]{2,1,0:T(8,128)(2,1)} %triple_hbm.1, bf16[1,1024,1024]{2,1,0:T(8,128)(2,1)} %output_hbm.1, bf16[1,1024,128]{2,1,0:T(8,128)(2,1)} %expand_hbm.1, bf16[1,128,1024]{2,1,0:T(8,128)(2,1)} %reduce_hbm.1, f32[1,1024]{1,0:T(1,128)} %again_ref.1, ...), custom_call_target="tpu_custom_call" | custom-call | tf_op jit(solution)/shard_map/pallas_call | solution.py:574
  114.7 1.3 %copy.11 = f32[3,256]{1,0:T(4,128)} copy(f32[3,256]{1,0:T(4,128)} %shard_map.91) | data formatting | bytes 6144

commit v6 on v5

--- a/solution.py
+++ b/solution.py
@@ -12,6 +12,8 @@
 ROWS = 197
 PAD = 208
 SENT = 200
+BLOCKS = 2
+WIDE = 1024 // BLOCKS
 D = 1024
 FF = 4096
 NF = 3
@@ -76,7 +78,7 @@
         (seg, lane_at(cx + 1, cz, core)), (seg, lane_at(cx + 3, cz, core)),
         (seg, lane_at(cx, cz + 1, core)), (seg, lane_at(cx, cz + 3, core)),
         (seg, lane_at(cx, cz, 1 - core)),
-        ((seg + 1) % 4, lane), ((seg + 2) % 4, lane), ((seg + 3) % 4, lane),
+        ((seg + 1) % 4, lane), ((seg + 3) % 4, lane),
     ]
     barrier = pltpu.get_barrier_semaphore()
     for peer in peers:
@@ -146,9 +148,13 @@
                     ready(kind)
                 for sign in (1, -1):
                     go(hop, kind, 0, 0, None, True, sign)
+                if ready is not None:
+                    for sign in (1, -1):
+                        go(hop, kind, 0, 0, None, False, sign)
             for kind in range(2):
-                for sign in (1, -1):
-                    go(hop, kind, 0, 0, None, False, sign)
+                if ready is None:
+                    for sign in (1, -1):
+                        go(hop, kind, 0, 0, None, False, sign)
                 go(sibling, kind, 0, 0)
 
         def spread(kind, dp):
@@ -293,15 +299,15 @@
             if at + 256 < depth:
                 wide = dot(act[...], exp_ref[:, at + 256:at + 512])
             hid[:, at:at + 256] = hidden
-        for c in range(4):
-            cols = slice(256 * c, 256 * c + 256)
+        for c in range(BLOCKS):
+            cols = slice(WIDE * c, WIDE * c + WIDE)
             emit(c, cols, state[f, :, cols] + dot(hid[:, 0:depth], red_ref[:, cols]))
 
     for copy in loads:
         copy.wait()
 
     def relay(f, c, way, section):
-        cols = slice(256 * c, 256 * c + 256)
+        cols = slice(WIDE * c, WIDE * c + WIDE)
         return pltpu.make_async_remote_copy(
             src_ref=outb.at[f, 0:SENT, cols], dst_ref=inb.at[way, f, 0:SENT, cols],
             send_sem=rel_send.at[f, c], recv_sem=rel_recv.at[way, f, c],
@@ -403,7 +409,7 @@
     @pl.when((seg == 1) | (seg == 2))
     def _():
         def step(f, carry):
-            for c in range(4):
+            for c in range(BLOCKS):
                 relay(f, c, 0, 2).wait_recv()
 
             @pl.when(seg == 2)
@@ -412,7 +418,7 @@
 
             @pl.when(seg == 1)
             def _():
-                for c in range(4):
+                for c in range(BLOCKS):
                     relay(f, c, 1, 2).wait_recv()
                 state[f] = inb[0, f].astype(F32) + inb[1, f].astype(F32)
 
@@ -534,7 +540,7 @@
     @pl.when(seg < 2)
     def _():
         for f in range(NF):
-            for c in range(4):
+            for c in range(BLOCKS):
                 relay(f, c, 0, 1).wait_send()
 
     @pl.when(seg == 0)
@@ -545,7 +551,7 @@
     @pl.when(seg == 3)
     def _():
         for f in range(NF):
-            for c in range(4):
+            for c in range(BLOCKS):
                 relay(f, c, 1, 1).wait_send()
 
     @pl.when((seg == 0) & (core == 1))
@@ -587,7 +593,7 @@
             pltpu.VMEM((NF, 8, 128), F32), pltpu.VMEM((SLOTS, NF, 8, 128), F32), pltpu.VMEM((4, 8, 256), F32), pltpu.VMEM((8, 256), F32),
             dma((5,)), dma((2, 4, 4, 2)), dma((2, 4, 4, 2)), dma((2, 4, 4)), dma((2, 4, 4)),
             dma((2, 4, 4, 2)), dma((2, 4, 4, 2)), dma((2, 4, 4)), dma((2, 4, 4)),
-            dma((NF, 4)), dma((2, NF, 4)), dma((NF,)), dma((NF,)), dma((2,)), dma((2,)),
+            dma((NF, BLOCKS)), dma((2, NF, BLOCKS)), dma((NF,)), dma((NF,)), dma((2,)), dma((2,)),
             dma((NF, SLOTS)), dma((NF, SLOTS)), dma((3,)), dma(()),
         ],
         compiler_params=pltpu.CompilerParams(

time: 116 us -> 114 us (0.983)
  Pallas kernels: 115 us -> 113 us
    pallas_call x1, Pallas kernels: 115 us -> 113 us  [body(): pl.pallas_call(kernel, out_shape=jax.ShapeDtypeStruct((NF, 256), F32), in...]
where the time goes in v6:
time: 114 us
  Pallas kernels  113 us (99%)
  local copies, waits for them, and re-layouts  1.28 us (1%)
    pallas_call x1, Pallas kernels, body(): pl.pallas_call(kernel, out_shape=jax.ShapeDtypeStruct((NF, 256), F32), in...  113 us

profile of v6, /device:TPU:0, one launch (start us, length us, event | category | flops | bytes accessed | tf_op | source)
XLA Modules:
  0.0 114.3 jit_solution(731101341906528393)
XLA Ops:
  0.0 113.0 %shard_map.91 = f32[3,256]{1,0:T(4,128)} custom-call(bf16[3,197,1024]{2,1,0:T(8,128)(2,1)} %frames_hbm.1, bf16[1,1024,3072]{2,1,0:T(8,128)(2,1)} %triple_hbm.1, bf16[1,1024,1024]{2,1,0:T(8,128)(2,1)} %output_hbm.1, bf16[1,1024,128]{2,1,0:T(8,128)(2,1)} %expand_hbm.1, bf16[1,128,1024]{2,1,0:T(8,128)(2,1)} %reduce_hbm.1, f32[1,1024]{1,0:T(1,128)} %again_ref.1, ...), custom_call_target="tpu_custom_call" | custom-call | tf_op jit(solution)/shard_map/pallas_call | solution.py:580
  113.0 1.3 %copy.11 = f32[3,256]{1,0:T(4,128)} copy(f32[3,256]{1,0:T(4,128)} %shard_map.91) | data formatting | bytes 6144

commit v7 on v6

--- a/solution.py
+++ b/solution.py
@@ -303,8 +303,9 @@
             cols = slice(WIDE * c, WIDE * c + WIDE)
             emit(c, cols, state[f, :, cols] + dot(hid[:, 0:depth], red_ref[:, cols]))
 
-    for copy in loads:
-        copy.wait()
+    def loaded():
+        for copy in loads:
+            copy.wait()
 
     def relay(f, c, way, section):
         cols = slice(WIDE * c, WIDE * c + WIDE)
@@ -327,6 +328,7 @@
 
     @pl.when(halves)
     def _():
+        loaded()
         for f in range(NF):
             @pl.when(seg == 0)
             def _():
@@ -408,6 +410,8 @@
 
     @pl.when((seg == 1) | (seg == 2))
     def _():
+        loaded()
+
         def step(f, carry):
             for c in range(BLOCKS):
                 relay(f, c, 0, 2).wait_recv()

time: 114 us -> 113 us (level)
  Pallas kernels: 113 us -> 111 us
    pallas_call x1, Pallas kernels: 113 us -> 111 us  [body(): pl.pallas_call(kernel, out_shape=jax.ShapeDtypeStruct((NF, 256), F32), in...]
where the time goes in v7:
time: 113 us
  Pallas kernels  111 us (98%)
  local copies, waits for them, and re-layouts  1.28 us (1%)
    pallas_call x1, Pallas kernels, body(): pl.pallas_call(kernel, out_shape=jax.ShapeDtypeStruct((NF, 256), F32), in...  111 us

profile of v7, /device:TPU:0, one launch (start us, length us, event | category | flops | bytes accessed | tf_op | source)
XLA Modules:
  0.0 112.6 jit_solution(6240125213694752704)
XLA Ops:
  0.0 111.3 %shard_map.91 = f32[3,256]{1,0:T(4,128)} custom-call(bf16[3,197,1024]{2,1,0:T(8,128)(2,1)} %frames_hbm.1, bf16[1,1024,3072]{2,1,0:T(8,128)(2,1)} %triple_hbm.1, bf16[1,1024,1024]{2,1,0:T(8,128)(2,1)} %output_hbm.1, bf16[1,1024,128]{2,1,0:T(8,128)(2,1)} %expand_hbm.1, bf16[1,128,1024]{2,1,0:T(8,128)(2,1)} %reduce_hbm.1, f32[1,1024]{1,0:T(1,128)} %again_ref.1, ...), custom_call_target="tpu_custom_call" | custom-call | tf_op jit(solution)/shard_map/pallas_call | solution.py:584
  111.3 1.3 %copy.11 = f32[3,256]{1,0:T(4,128)} copy(f32[3,256]{1,0:T(4,128)} %shard_map.91) | data formatting | bytes 6144
